TPU v7x, 32 devices: a whole 2x2x4 slice. The times are simulated.
32 devices in a mesh: seq: 16 (over z, x, core), head: 2 (over y).
Axes of the slice: x: 2, y: 2, z: 4, core: 2. Of those that a mesh axis runs over, the one named last changes fastest.
Arguments:
- query_rows: bfloat16 [8192, 1024], P(('seq', 'head')), may hold values from -16 to 16
- key_rows: bfloat16 [8192, 1024], P(('seq', 'head')), may hold values from -16 to 16
- value_rows: bfloat16 [8192, 1024], P(('seq', 'head')), may hold values from -6 to 6
- out_grad: bfloat16 [8192, 1024], P(('seq', 'head')), may hold values from -6 to 6
- random_blocks: int32 [128, 2], P('seq'), may hold values from 0 to 127, as said below
- global_blocks: int32 [2], replicated, may hold values from 0 to 127
Outputs:
- attn_out: bfloat16 [8192, 1024], P(('seq', 'head'))
- q_grad: bfloat16 [8192, 1024], P(('seq', 'head'))
- k_grad: bfloat16 [8192, 1024], P(('seq', 'head'))
- v_grad: bfloat16 [8192, 1024], P(('seq', 'head'))
Inputs may be any that keep to these rules, and one draw needn't show every extreme that they name: `random_blocks`: the 16 random blocks named by the query blocks of one device belong to 16 different devices along `seq`: at most one of them lies among any one device's 8 blocks.
All inputs are finite; a program needn't handle non-finite values.
Results may differ from a plain program's by a relative error of at most 0.011.
Values may be sent and summed in bfloat16 or wider, within the bound.
A program may use at most 128 MiB of HBM per device.

v0:
```python
from functools import partial

import jax
import jax.numpy as jnp
from jax import lax
from jax.sharding import PartitionSpec as P

HEAD_DIM = 64
BLOCK = 64
RANDOM = 2
GLOBALS = 2


masked_score = -1e30


def extended(x, sides, width):
    for axis, dim in sides:
        peers, length = (lax.axis_size(axis), x.shape[dim])
        up = [(i, (i + 1) % peers) for i in range(peers - 1)]
        down = [(j, i) for i, j in up]
        last = lax.slice_in_dim(x, length - width, length, axis=dim)
        initial = lax.slice_in_dim(x, 0, width, axis=dim)
        before = lax.ppermute(last, axis, up)
        after = lax.ppermute(initial, axis, down)
        x = jnp.concatenate([before, x, after], axis=dim)
    return x


def shifted(value, axis, steps):
    count = lax.axis_size(axis)
    initial, last = (max(0, -steps), min(count, count - steps))
    return lax.ppermute(value, axis, [(source, source + steps) for source in range(initial, last)])


def slot_table(flat_ids, per_device, capacity):
    source = flat_ids // per_device
    within = flat_ids % per_device
    order = jnp.arange(flat_ids.shape[0], dtype=jnp.int32)
    earlier = (source[:, None] == source[None, :]) & (order[None, :] < order[:, None])
    rank = jnp.sum(earlier.astype(jnp.int32), axis=1)
    return (source * capacity + rank, within)


def attend_group(packed, scale_factor, width_here):
    query_group, pair_all, grad_group, key_ok = packed
    groups, block_rows = (query_group.shape[0], query_group.shape[1])
    key_count = pair_all.shape[1]
    head_count = width_here // HEAD_DIM
    query_heads = query_group.reshape(groups, block_rows, head_count, HEAD_DIM)
    grad_heads = grad_group.reshape(groups, block_rows, head_count, HEAD_DIM)
    key_heads = pair_all[:, :, :width_here].reshape(groups, key_count, head_count, HEAD_DIM)
    value_heads = pair_all[:, :, width_here:].reshape(groups, key_count, head_count, HEAD_DIM)
    scores = (
        jnp.einsum("gqhd,gkhd->ghqk", query_heads, key_heads, preferred_element_type=jnp.float32)
        * scale_factor
    )
    scores = jnp.where(key_ok[:, None, None, :], scores, masked_score)
    row_max = jnp.max(scores, axis=-1, keepdims=True)
    weights_raw = jnp.exp(scores - row_max)
    probabilities = weights_raw / jnp.sum(weights_raw, axis=-1, keepdims=True)
    probs_half = probabilities.astype(jnp.bfloat16)
    attended = jnp.einsum(
        "ghqk,gkhd->gqhd", probs_half, value_heads, preferred_element_type=jnp.float32
    )
    prob_grad = jnp.einsum(
        "gqhd,gkhd->ghqk", grad_heads, value_heads, preferred_element_type=jnp.float32
    )
    row_delta = jnp.sum(grad_heads.astype(jnp.float32) * attended, axis=-1).transpose(0, 2, 1)[
        ..., None
    ]
    score_grad = (probabilities * (prob_grad - row_delta)).astype(jnp.bfloat16)
    query_grad = (
        jnp.einsum("ghqk,gkhd->gqhd", score_grad, key_heads, preferred_element_type=jnp.float32)
        * scale_factor
    )
    key_grad = (
        jnp.einsum("ghqk,gqhd->gkhd", score_grad, query_heads, preferred_element_type=jnp.float32)
        * scale_factor
    )
    value_grad = jnp.einsum(
        "ghqk,gqhd->gkhd", probs_half, grad_heads, preferred_element_type=jnp.float32
    )
    pair_grad = jnp.concatenate(
        [
            key_grad.reshape(groups, key_count, width_here),
            value_grad.reshape(groups, key_count, width_here),
        ],
        axis=-1,
    )
    pair_grad = pair_grad.reshape(groups, key_count // block_rows, block_rows, 2 * width_here)
    window_part = pair_grad[:, 0:3]
    random_part = pair_grad[:, 3 : 3 + RANDOM].astype(jnp.bfloat16)
    global_part = jnp.sum(pair_grad[:, 3 + RANDOM :], axis=0)
    attended_half = attended.reshape(groups, block_rows, width_here).astype(jnp.bfloat16)
    query_half = query_grad.reshape(groups, block_rows, width_here).astype(jnp.bfloat16)
    return (attended_half, query_half, window_part, random_part, global_part)


def body(query_rows, key_rows, value_rows, out_grad, random_blocks, global_blocks):
    query_here, key_here, value_here, grad_here = (
        lax.all_to_all(query_rows, "head", split_axis=1, concat_axis=0, tiled=True),
        lax.all_to_all(key_rows, "head", split_axis=1, concat_axis=0, tiled=True),
        lax.all_to_all(value_rows, "head", split_axis=1, concat_axis=0, tiled=True),
        lax.all_to_all(out_grad, "head", split_axis=1, concat_axis=0, tiled=True),
    )
    tokens_here, width_here = query_here.shape
    blocks_here = tokens_here // BLOCK
    seq_devices = lax.axis_size("seq")
    my_index = lax.axis_index("seq")
    capacity = max(1, RANDOM * blocks_here // seq_devices)
    slot_total = seq_devices * capacity
    request_total = RANDOM * blocks_here
    scale_factor = HEAD_DIM ** (-0.5)
    pair_rows = jnp.concatenate([key_here, value_here], axis=1)
    pair_blocks = pair_rows.reshape(blocks_here, BLOCK, 2 * width_here)
    padded = extended(pair_rows, (("seq", 0),), BLOCK)
    padded_blocks = padded.reshape(blocks_here + 2, BLOCK, 2 * width_here)
    window_rows = jnp.stack(
        [
            padded_blocks[0:blocks_here],
            padded_blocks[1 : blocks_here + 1],
            padded_blocks[2 : blocks_here + 2],
        ],
        axis=1,
    )
    flat_ids = random_blocks.reshape(request_total)
    slot_of, within_of = slot_table(flat_ids, blocks_here, capacity)
    slot_iota = jnp.arange(slot_total, dtype=jnp.int32)
    slot_hit = slot_of[:, None] == slot_iota[None, :]
    asked_for = jnp.sum(jnp.where(slot_hit, within_of[:, None], 0), axis=0).reshape(
        seq_devices, capacity
    )
    served = lax.all_to_all(asked_for, "seq", split_axis=0, concat_axis=0, tiled=True)
    served_flat = served.reshape(slot_total)
    outgoing = jnp.take(pair_blocks, served_flat, axis=0).reshape(
        seq_devices, capacity, BLOCK, 2 * width_here
    )
    incoming = lax.all_to_all(outgoing, "seq", split_axis=0, concat_axis=0, tiled=True).reshape(
        slot_total, BLOCK, 2 * width_here
    )
    picked = jnp.take(incoming, slot_of, axis=0).reshape(blocks_here, RANDOM, BLOCK, 2 * width_here)
    owners = global_blocks // blocks_here
    owned_at = global_blocks % blocks_here
    pieces = jnp.take(pair_blocks, owned_at, axis=0).astype(jnp.float32)
    held = (owners == my_index)[:, None, None]
    global_pair = lax.psum(jnp.where(held, pieces, 0.0), "seq").astype(jnp.bfloat16)
    global_every = jnp.broadcast_to(
        global_pair[None], (blocks_here, GLOBALS, BLOCK, 2 * width_here)
    )
    pair_all = jnp.concatenate([window_rows, picked, global_every], axis=1).reshape(
        blocks_here, -1, 2 * width_here
    )
    block_number = my_index * blocks_here + jnp.arange(blocks_here, dtype=jnp.int32)
    total_blocks = blocks_here * seq_devices
    part_ok = jnp.ones((blocks_here, 3 + RANDOM + GLOBALS), jnp.bool_)
    part_ok = part_ok.at[:, 0].set(block_number > 0).at[:, 2].set(block_number < total_blocks - 1)
    key_ok = jnp.repeat(part_ok, BLOCK, axis=1)
    group_size = min(blocks_here, max(1, 512 // BLOCK))
    group_count = blocks_here // group_size

    def regroup(tensor):
        return tensor.reshape((group_count, group_size) + tensor.shape[1:])

    packed = (
        regroup(query_here.reshape(blocks_here, BLOCK, width_here)),
        regroup(pair_all),
        regroup(grad_here.reshape(blocks_here, BLOCK, width_here)),
        regroup(key_ok),
    )
    attended, query_grad, window_grad, random_grad, global_grad = lax.map(
        partial(attend_group, scale_factor=scale_factor, width_here=width_here), packed
    )
    attended = attended.reshape(tokens_here, width_here)
    query_grad = query_grad.reshape(tokens_here, width_here)
    window_grad = window_grad.reshape(blocks_here, 3, BLOCK, 2 * width_here)
    window_sum = (
        jnp.pad(window_grad[:, 0], ((0, 2), (0, 0), (0, 0)))
        + jnp.pad(window_grad[:, 1], ((1, 1), (0, 0), (0, 0)))
        + jnp.pad(window_grad[:, 2], ((2, 0), (0, 0), (0, 0)))
    )
    from_above = shifted(window_sum[0].astype(jnp.bfloat16), "seq", -1).astype(jnp.float32)
    from_below = shifted(window_sum[blocks_here + 1].astype(jnp.bfloat16), "seq", 1).astype(
        jnp.float32
    )
    owned_grad = window_sum[1 : blocks_here + 1]
    owned_grad = owned_grad.at[blocks_here - 1].add(from_above).at[0].add(from_below)
    random_flat = random_grad.reshape(request_total, BLOCK, 2 * width_here)
    slot_used = jnp.any(slot_hit, axis=0)
    source_request = jnp.sum(
        jnp.where(slot_hit, jnp.arange(request_total, dtype=jnp.int32)[:, None], 0), axis=0
    )
    sending = jnp.where(
        slot_used[:, None, None],
        jnp.take(random_flat, source_request, axis=0),
        jnp.zeros((), jnp.bfloat16),
    )
    sending = sending.reshape(seq_devices, capacity, BLOCK, 2 * width_here)
    returned = lax.all_to_all(sending, "seq", split_axis=0, concat_axis=0, tiled=True).reshape(
        slot_total, BLOCK * 2 * width_here
    )
    owner_hit = (served_flat[None, :] == jnp.arange(blocks_here, dtype=jnp.int32)[:, None]).astype(
        jnp.bfloat16
    )
    owned_grad = owned_grad + jnp.dot(
        owner_hit, returned, preferred_element_type=jnp.float32
    ).reshape(blocks_here, BLOCK, 2 * width_here)
    global_total = lax.psum(jnp.sum(global_grad, axis=0), "seq")
    block_iota = jnp.arange(blocks_here, dtype=jnp.int32)
    for global_slot in range(GLOBALS):
        hit_mask = (block_iota == owned_at[global_slot]) & (owners[global_slot] == my_index)
        owned_grad = owned_grad + jnp.where(
            hit_mask[:, None, None], global_total[global_slot][None], 0.0
        )
    pair_grad = owned_grad.reshape(tokens_here, 2 * width_here).astype(jnp.bfloat16)
    return (
        lax.all_to_all(attended, "head", split_axis=0, concat_axis=1, tiled=True),
        lax.all_to_all(query_grad, "head", split_axis=0, concat_axis=1, tiled=True),
        lax.all_to_all(pair_grad[:, :width_here], "head", split_axis=0, concat_axis=1, tiled=True),
        lax.all_to_all(pair_grad[:, width_here:], "head", split_axis=0, concat_axis=1, tiled=True),
    )


def solution(mesh):
    placed = (
        P(("seq", "head"), None),
        P(("seq", "head"), None),
        P(("seq", "head"), None),
        P(("seq", "head"), None),
        P("seq", None),
        P(),
    )
    return jax.shard_map(
        body,
        mesh=mesh,
        in_specs=placed,
        out_specs=(
            P(("seq", "head"), None),
            P(("seq", "head"), None),
            P(("seq", "head"), None),
            P(("seq", "head"), None),
        ),
        check_vma=False,
    )
```

profile of v0, /device:TPU:0, one launch (start us, length us, event | category | flops | bytes accessed | tf_op | source)
XLA Modules:
  0.0 468.4 jit_solution(2253730301342176993)
XLA Ops:
  9.6 7.4 %all-to-all-start.2 = ((s32[16,1,1]{2,1,0:T(1,128)}), s32[16,1,1]{2,1,0:T(1,128)S(1)}, u32[]{:S(2)}, u32[]{:S(2)}) async-start(s32[16,1,1]{2,1,0:T(1,128)} %copy.174), calls=%async_computation.2 | async-start | bytes 16384 | tf_op jit(solution)/shard_map/all_to_all | solution.py:134
  17.0 2.1 copy.169
  19.1 4.2 all-to-all-done.2
  23.3 3.5 all-to-all-start.1
  28.9 6.1 %all-to-all-done.1 = bf16[256,2,512]{0,2,1:T(8,128)(2,1)S(1)} async-done(((bf16[256,2,512]{0,2,1:T(8,128)(2,1)}), bf16[256,2,512]{0,2,1:T(8,128)(2,1)S(1)}, u32[]{:S(2)}, u32[]{:S(2)}) %all-to-all-start.1) | async-done | bytes 524320 | tf_op jit(solution)/shard_map/all_to_all | solution.py:104
  35.0 3.5 all-to-all-start
  40.6 5.3 %all-to-all-done = bf16[256,2,512]{0,2,1:T(8,128)(2,1)S(1)} async-done(((bf16[256,2,512]{0,2,1:T(8,128)(2,1)}), bf16[256,2,512]{0,2,1:T(8,128)(2,1)S(1)}, u32[]{:S(2)}, u32[]{:S(2)}) %all-to-all-start) | async-done | bytes 524320 | tf_op jit(solution)/shard_map/all_to_all | solution.py:103
  45.8 3.5 all-to-all-start.4
  51.9 4.0 all-to-all-done.4
  55.9 3.5 all-to-all-start.6
  59.4 3.2 fusion.23
  62.6 3.4 all-to-all-done.6
  66.0 4.4 all-to-all-start.3
  77.1 3.7 collective-permute-start
  81.5 84.3 %all-reduce.8 = bf16[2,64,1024]{2,1,0:T(8,128)(2,1)S(1)} all-reduce(f32[2,64,1024]{2,1,0:T(8,128)S(1)} %convert_select_fusion), channel_id=1, replica_groups=mesh['seq'=16,'head'=2] {'seq'}, use_global_device_ids=true, to_apply=%region_2.4 | all-reduce | flops 131072 | bytes 786432 | tf_op jit(solution)/shard_map/psum | solution.py:147
  167.1 2.4 reshape.419
  175.9 3.6 gather_fusion.2
  184.5 6.7 %fusion.45 = (bf16[8,448,512]{2,1,0:T(8,128)(2,1)}, bf16[8,448,512]{2,1,0:T(8,128)(2,1)}) fusion(bf16[8,448,1024]{2,1,0:T(8,128)(2,1)} %bitcast.21), kind=kLoop, calls=%fused_computation.124 | loop fusion | bytes 14680064 | tf_op jit(solution)/shard_map/while/body/eval_jaxpr/slice | solution.py:52
  191.2 6.3 %copy.181 = bf16[8,448,512]{1,2,0:T(8,128)(2,1)} copy(bf16[8,448,512]{2,1,0:T(8,128)(2,1)} %get-tuple-element.113) | data formatting | bytes 7340032 | tf_op jit(solution)/shard_map/while/body/eval_jaxpr/slice | solution.py:53
  197.5 6.3 %copy.182 = bf16[8,448,512]{1,2,0:T(8,128)(2,1)} copy(bf16[8,448,512]{2,1,0:T(8,128)(2,1)} %get-tuple-element.112) | data formatting | bytes 7340032 | tf_op jit(solution)/shard_map/while/body/eval_jaxpr/slice | solution.py:52
  203.8 8.5 %fusion.49 = (f32[8,8,64]{2,1,0:T(8,128)S(1)}, f32[8,8,64,448]{3,2,1,0:T(8,128)}) fusion(pred[8,448]{1,0:T(8,128)(4,1)S(1)} %copy-done.8, bf16[8,64,8,64]{1,3,2,0:T(8,128)(2,1)S(1)} %copy.192, bf16[8,448,8,64]{1,3,2,0:T(8,128)(2,1)} %bitcast.153), kind=kOutput, calls=%fused_computation.128 | convolution fusion | flops 242221504 | bytes 11554304 | tf_op jit(solution)/shard_map/while/body/eval_jaxpr/sub | solution.py:60
  212.3 4.0 fusion.12
  217.0 2.2 bitcast_convert_fusion
  219.2 4.5 convolution_bitcast_fusion
  224.2 2.4 fusion.1
  228.6 4.5 multiply_bitcast_fusion
  233.1 13.2 %reshape.467 = f32[8,7,64,512]{2,1,3,0:T(8,128)} reshape(f32[8,448,8,64]{1,3,2,0:T(8,128)} %multiply_bitcast_fusion) | data formatting | bytes 14680064 | tf_op jit(solution)/shard_map/while/body/eval_jaxpr/concatenate | solution.py:84
  246.3 12.2 %copy.196 = f32[8,7,64,512]{3,2,0,1:T(8,128)} copy(f32[8,7,64,512]{2,1,3,0:T(8,128)} %reshape.467) | data formatting | bytes 14680064 | tf_op jit(solution)/shard_map/while/body/eval_jaxpr/concatenate | solution.py:84
  258.4 13.2 %reshape.468 = f32[8,7,64,512]{2,1,3,0:T(8,128)} reshape(f32[8,448,8,64]{1,3,2,0:T(8,128)} %convolution_bitcast_fusion) | data formatting | bytes 14680064 | tf_op jit(solution)/shard_map/while/body/eval_jaxpr/concatenate | solution.py:84
  271.6 12.2 %copy.197 = f32[8,7,64,512]{3,2,0,1:T(8,128)} copy(f32[8,7,64,512]{2,1,3,0:T(8,128)} %reshape.468) | data formatting | bytes 14680064 | tf_op jit(solution)/shard_map/while/body/eval_jaxpr/concatenate | solution.py:84
  283.8 2.5 fusion.7
  287.9 2.3 gather_fusion.3
  291.8 4.5 all-to-all-start.8
  299.6 3.5 fusion.14
  303.1 2.4 fusion.44
  314.8 2.6 collective-permute-start.3
  317.4 3.4 fusion.8
  321.9 2.6 copy.199
  324.8 6.3 %scatter-add.9 = f32[8,64,1024]{2,0,1:T(8,128)} dynamic-update-slice(f32[8,64,1024]{2,0,1:T(8,128)} %copy.199, f32[1,64,1024]{2,0,1:T(1,128)S(1)} %copy_add_fusion, s32[]{:T(128)} %constant.223.clone.1, s32[]{:T(128)} %constant.223.clone.1, s32[]{:T(128)} %constant.223.clone.1) | dynamic-update-slice | bytes 524292 | tf_op jit(solution)/shard_map/scatter-add | solution.py:187
  331.2 84.8 %all-reduce.7.cloned.1.call-done = f32[2,64,1024]{2,1,0:T(8,128)} async-done(((f32[2,64,1024]{2,1,0:T(8,128)}), f32[2,64,1024]{2,1,0:T(8,128)}) %all-reduce.7.cloned.1.call-update) | async-done | bytes 524304 | tf_op jit(solution)/shard_map/psum | solution.py:208
  417.0 3.5 all-to-all-start.5
  420.6 3.7 add_convert_fusion
  424.9 4.5 all-to-all-done.5
  429.3 3.5 all-to-all-start.7
  433.7 7.1 %all-to-all-done.7 = bf16[2,256,512]{2,1,0:T(8,128)(2,1)S(1)} async-done(((bf16[2,256,512]{2,1,0:T(8,128)(2,1)}), bf16[2,256,512]{2,1,0:T(8,128)(2,1)S(1)}, u32[]{:S(2)}, u32[]{:S(2)}) %all-to-all-start.7) | async-done | bytes 524320 | tf_op jit(solution)/shard_map/all_to_all | solution.py:218
  440.8 9.5 %all_to_all.165 = bf16[2,256,512]{2,1,0:T(8,128)(2,1)S(1)} all-to-all(bf16[2,256,512]{2,1,0:T(8,128)(2,1)S(1)} %bitcast.185), channel_id=1, replica_groups=mesh['seq'=16,'head'=2] {'head'}, dimensions={0} | all-to-all | bytes 1048576 | tf_op jit(solution)/shard_map/all_to_all | solution.py:219
  450.3 3.5 all-to-all-start.10
  457.4 2.9 all-to-all-done.10
  (119 shorter events, 55.3 us)
Async XLA Ops:
  7.2 31.3 %copy-start.6 = (bf16[256,1024]{1,0:T(8,128)(2,1)S(1)}, bf16[256,1024]{1,0:T(8,128)(2,1)}, u32[]{:S(2)}) copy-start(bf16[256,1024]{1,0:T(8,128)(2,1)} %param.16) | copy-start | bytes 1572868
  9.6 13.8 %all-to-all-start.2 = ((s32[16,1,1]{2,1,0:T(1,128)}), s32[16,1,1]{2,1,0:T(1,128)S(1)}, u32[]{:S(2)}, u32[]{:S(2)}) async-start(s32[16,1,1]{2,1,0:T(1,128)} %copy.174), calls=%async_computation.2 | async-start | bytes 16384 | tf_op jit(solution)/shard_map/all_to_all | solution.py:134
  17.0 22.4 %copy-start.7 = (bf16[256,1024]{1,0:T(8,128)(2,1)S(1)}, bf16[256,1024]{1,0:T(8,128)(2,1)}, u32[]{:S(2)}) copy-start(bf16[256,1024]{1,0:T(8,128)(2,1)} %param.19) | copy-start | bytes 1572868
  23.3 11.7 %all-to-all-start.1 = ((bf16[256,2,512]{0,2,1:T(8,128)(2,1)}), bf16[256,2,512]{0,2,1:T(8,128)(2,1)S(1)}, u32[]{:S(2)}, u32[]{:S(2)}) async-start(bf16[256,2,512]{0,2,1:T(8,128)(2,1)} %bitcast.3), calls=%async_computation.1 | async-start | bytes 1048576 | tf_op jit(solution)/shard_map/all_to_all | solution.py:104
  35.0 10.8 %all-to-all-start = ((bf16[256,2,512]{0,2,1:T(8,128)(2,1)}), bf16[256,2,512]{0,2,1:T(8,128)(2,1)S(1)}, u32[]{:S(2)}, u32[]{:S(2)}) async-start(bf16[256,2,512]{0,2,1:T(8,128)(2,1)} %bitcast), calls=%async_computation | async-start | bytes 1048576 | tf_op jit(solution)/shard_map/all_to_all | solution.py:103
  40.6 9.4 %copy-start.12 = (s32[16]{0:T(128)}, s32[16]{0:T(128)S(1)}, u32[]{:S(2)}) copy-start(s32[16]{0:T(128)S(1)} %reduce.18) | copy-start | bytes 196
  45.8 10.1 %all-to-all-start.4 = ((bf16[256,2,512]{2,0,1:T(8,128)(2,1)}), bf16[256,2,512]{2,0,1:T(8,128)(2,1)S(1)}, u32[]{:S(2)}, u32[]{:S(2)}) async-start(bf16[256,2,512]{2,0,1:T(8,128)(2,1)} %bitcast.152), calls=%async_computation.4 | async-start | bytes 1048576 | tf_op jit(solution)/shard_map/all_to_all | solution.py:102
  55.9 10.1 %all-to-all-start.6 = ((bf16[256,2,512]{2,0,1:T(8,128)(2,1)}), bf16[256,2,512]{2,0,1:T(8,128)(2,1)S(1)}, u32[]{:S(2)}, u32[]{:S(2)}) async-start(bf16[256,2,512]{2,0,1:T(8,128)(2,1)} %bitcast.175), calls=%async_computation.6 | async-start | bytes 1048576 | tf_op jit(solution)/shard_map/all_to_all | solution.py:105
  62.6 11.3 %copy-start.14 = (s32[2]{0:T(128)S(1)}, s32[2]{0:T(128)}, u32[]{:S(2)}) copy-start(s32[2]{0:T(128)} %param.21) | copy-start | bytes 28
  66.0 9.9 %copy-start.5 = (bf16[256,2,512]{2,0,1:T(8,128)(2,1)}, bf16[256,2,512]{2,0,1:T(8,128)(2,1)S(1)}, u32[]{:S(2)}) copy-start(bf16[256,2,512]{2,0,1:T(8,128)(2,1)S(1)} %all-to-all-done.6) | copy-start | bytes 1572868
  66.0 109.9 %all-to-all-start.3 = ((bf16[16,1,64,1024]{3,2,1,0:T(8,128)(2,1)}), bf16[16,1,64,1024]{3,2,1,0:T(8,128)(2,1)}, u32[]{:S(2)}, u32[]{:S(2)}) async-start(bf16[16,1,64,1024]{3,2,1,0:T(8,128)(2,1)} %fusion.23), calls=%async_computation.3 | async-start | bytes 4194304 | tf_op jit(solution)/shard_map/all_to_all | solution.py:139
  75.9 95.4 %collective-permute-start.1 = (bf16[64,1024]{1,0:T(8,128)(2,1)}, bf16[64,1024]{1,0:T(8,128)(2,1)}, u32[]{:S(2)}, u32[]{:S(2)}) collective-permute-start(bf16[64,1024]{1,0:T(8,128)(2,1)} %get-tuple-element.120), channel_id=1, source_target_pairs={{2,0},{4,2},{6,4},{8,6},{10,8},{12,10},{14,12},{16,14},{18,16},{20... | collective-permute-start | bytes 393224 | tf_op jit(solution)/shard_map/ppermute | solution.py:25
  77.1 94.1 %collective-permute-start = (bf16[64,1024]{1,0:T(8,128)(2,1)S(1)}, bf16[64,1024]{1,0:T(8,128)(2,1)}, u32[]{:S(2)}, u32[]{:S(2)}) collective-permute-start(bf16[64,1024]{1,0:T(8,128)(2,1)S(1)} %get-tuple-element.121), channel_id=1, source_target_pairs={{0,2},{2,4},{4,6},{6,8},{8,10},{10,12},{12,14},{14,16},{16,18},{18... | collective-permute-start | bytes 393224 | tf_op jit(solution)/shard_map/ppermute | solution.py:24
  175.9 3.6 copy-start.9
  197.5 6.3 %copy-start.8 = (pred[8,448]{1,0:T(8,128)(4,1)S(1)}, pred[8,448]{1,0:T(8,128)(4,1)}, u32[]{:S(2)}) copy-start(pred[8,448]{1,0:T(8,128)(4,1)} %broadcast_in_dim.183) | copy-start | bytes 10756
  212.3 4.6 copy-start.3
  217.0 7.2 %slice-start = ((s8[8388608]{0:T(1024)(128)(4,1)}), s8[4194304]{0:T(1024)(128)(4,1)S(1)}, s32[]{:S(2)}) async-start(s8[8388608]{0:T(1024)(128)(4,1)} %bitcast.165), calls=%async_computation.12 | async-start | bytes 8388608
  219.2 5.0 %slice-start.1 = ((s8[8388608]{0:T(1024)(128)(4,1)}), s8[4194304]{0:T(1024)(128)(4,1)S(1)}, s32[]{:S(2)}) async-start(s8[8388608]{0:T(1024)(128)(4,1)} %bitcast.165), calls=%async_computation.13 | async-start | bytes 8388608
  226.6 2.0 copy-start
  287.9 2.3 copy-start.10
  287.9 2.3 copy-start.11
  291.8 125.2 %all-to-all-start.8 = ((bf16[16,1,64,1024]{3,2,1,0:T(8,128)(2,1)}), bf16[16,1,64,1024]{3,2,1,0:T(8,128)(2,1)}, u32[]{:S(2)}, u32[]{:S(2)}) async-start(bf16[16,1,64,1024]{3,2,1,0:T(8,128)(2,1)} %fusion.24), calls=%async_computation.8 | async-start | bytes 4194304 | tf_op jit(solution)/shard_map/all_to_all | solution.py:199
  296.3 119.7 %all-reduce.7.cloned.1.call-start = ((), (), s32[]{:S(2)}) async-start(), calls=%async_computation.11 | async-start | bytes 1048576 | tf_op jit(solution)/shard_map/psum | solution.py:208
  303.1 4.0 copy-start.1
  303.1 4.4 copy-start.2
  305.5 3.3 copy-start.4
  305.5 15.4 %collective-permute-start.2 = (bf16[64,1024]{1,0:T(8,128)(2,1)S(1)}, bf16[64,1024]{1,0:T(8,128)(2,1)S(1)}, u32[]{:S(2)}, u32[]{:S(2)}) collective-permute-start(bf16[64,1024]{1,0:T(8,128)(2,1)S(1)} %get-tuple-element.115), channel_id=1, source_target_pairs={{2,0},{4,2},{6,4},{8,6},{10,8},{12,10},{14,12},{16,14},{18,16},{20... | collective-permute-start | bytes 393224 | tf_op jit(solution)/shard_map/ppermute | solution.py:33
  314.8 9.7 %collective-permute-start.3 = (bf16[64,1024]{1,0:T(8,128)(2,1)S(1)}, bf16[64,1024]{1,0:T(8,128)(2,1)S(1)}, u32[]{:S(2)}, u32[]{:S(2)}) collective-permute-start(bf16[64,1024]{1,0:T(8,128)(2,1)S(1)} %get-tuple-element.114), channel_id=1, source_target_pairs={{0,2},{2,4},{4,6},{6,8},{8,10},{10,12},{12,14},{14,16},{16,18},{18... | collective-permute-start | bytes 393224 | tf_op jit(solution)/shard_map/ppermute | solution.py:33
  324.4 96.1 %copy-start.13 = (s32[16]{0:T(128)S(1)}, s32[16]{0:T(128)}, u32[]{:S(2)}) copy-start(s32[16]{0:T(128)} %copy-done.12) | copy-start | bytes 196
  417.0 12.3 %all-to-all-start.5 = ((bf16[2,256,512]{2,1,0:T(8,128)(2,1)}), bf16[2,256,512]{2,1,0:T(8,128)(2,1)S(1)}, u32[]{:S(2)}, u32[]{:S(2)}) async-start(bf16[2,256,512]{2,1,0:T(8,128)(2,1)} %convert_element_type.72), calls=%async_computation.5 | async-start | bytes 1048576 | tf_op jit(solution)/shard_map/all_to_all | solution.py:217
  429.3 11.4 %all-to-all-start.7 = ((bf16[2,256,512]{2,1,0:T(8,128)(2,1)}), bf16[2,256,512]{2,1,0:T(8,128)(2,1)S(1)}, u32[]{:S(2)}, u32[]{:S(2)}) async-start(bf16[2,256,512]{2,1,0:T(8,128)(2,1)} %convert_element_type.77), calls=%async_computation.7 | async-start | bytes 1048576 | tf_op jit(solution)/shard_map/all_to_all | solution.py:218
  450.3 10.1 %all-to-all-start.10 = ((bf16[2,256,512]{2,1,0:T(8,128)(2,1)}), bf16[2,256,512]{2,1,0:T(8,128)(2,1)S(1)}, u32[]{:S(2)}, u32[]{:S(2)}) async-start(bf16[2,256,512]{2,1,0:T(8,128)(2,1)} %bitcast.58), calls=%async_computation.10 | async-start | bytes 1048576 | tf_op jit(solution)/shard_map/all_to_all | solution.py:220
Sparse Core Ops, SparseCore 0:
  321.0 94.9 all-reduce.6
where the time goes:
time: 471 us; the launch traced here: 468 us
  local copies, waits for them, and re-layouts  125 us (27%)
  waiting for transfers between devices  122 us (26%)
  blocking collectives  93.7 us (20%)
  starting transfers between devices  49.9 us (11%)
  other arithmetic  34 us (7%)
  matrix products  27.1 us (6%)
  between operations  15.9 us (3%)
    psum x1, waiting for transfers between devices, body(): global_total = lax.psum(jnp.sum(global_grad, axis=0), 'seq')  84.8 us
    psum x1, blocking collectives, body(): lax.psum(jnp.where(held, pieces, 0.0), 'seq').astype(jnp.bfloat16)  84.3 us
    concatenate x4, local copies, waits for them, and re-layouts, attend_group(): jnp.concatenate([key_grad.reshape(groups, key_count, width_here), value_g...  50.6 us
    unnamed x44, local copies, waits for them, and re-layouts  15.8 us
    slice x2, local copies, waits for them, and re-layouts, attend_group(): pair_all[:, :, :width_here].reshape(groups, key_count, head_count, HEAD_DIM)  13 us
    all_to_all x1, blocking collectives, body(): lax.all_to_all(pair_grad[:, :width_here], 'head', split_axis=0, concat_ax...  9.49 us
  transfers between devices with their start and end apart: 15, of which 9 were waited for; matrix products, arithmetic and copies ran while one was open for 14% of the time, Pallas kernels for 0%

commit v1 on v0

v1 whole, which is shorter than its diff:
```python
from functools import partial

import jax
import jax.numpy as jnp
from jax import lax
from jax.experimental import pallas as pl
from jax.experimental.pallas import tpu as pltpu
from jax.sharding import PartitionSpec as P

HEAD_DIM = 64
BLOCK = 64
RANDOM = 2
GLOBALS = 2
PARTS = 3 + RANDOM + GLOBALS
MASKED = -1e30
MESH = pl.DeviceIdType.MESH
VMEM = pl.BlockSpec(memory_space=pltpu.VMEM)
SMEM = pl.BlockSpec(memory_space=pltpu.SMEM)


def params(cid):
    return pltpu.CompilerParams(
        collective_id=cid, has_side_effects=True, vmem_limit_bytes=48 * 1024 * 1024
    )


def greet(n, heads):
    s, h = lax.axis_index("seq"), lax.axis_index("head")
    barrier = pltpu.get_barrier_semaphore()
    if n > 0:

        def hello(d, c):
            pl.semaphore_signal(
                barrier, inc=1, device_id={"seq": lax.rem(s + d, n)}, device_id_type=MESH
            )
            return c

        lax.fori_loop(1, n, hello, 0)
    for d in range(1, heads):
        pl.semaphore_signal(
            barrier, inc=1, device_id={"head": lax.rem(h + d, heads)}, device_id_type=MESH
        )
    pl.semaphore_wait(barrier, max(n - 1, 0) + heads - 1)


def cols(index, width, base=0):
    return pl.ds(pl.multiple_of(base + index * width, 128), width)


def rows(index, count):
    return pl.ds(pl.multiple_of(index * count, 16), count)


def each(n, f):
    def step(d, c):
        f(d)
        return c

    lax.fori_loop(1, n, step, 0)


def exchange(views, heads, send, recv, local):
    h = lax.axis_index("head")
    copies, own = [], []
    for k, view in enumerate(views):
        for d in range(1, heads):
            peer = lax.rem(h + d, heads)
            source, target = view(h, peer)
            at = k * heads + d
            copies.append(
                pltpu.make_async_remote_copy(
                    src_ref=source,
                    dst_ref=target,
                    send_sem=send.at[at],
                    recv_sem=recv.at[at],
                    device_id={"head": peer},
                    device_id_type=MESH,
                )
            )
        source, target = view(h, h)
        own.append(pltpu.make_async_copy(source, target, local.at[k]))
    return copies, own


def to_heads(src, dst, tokens, width, base=0):
    return lambda a, b: (src.at[:, cols(b, width)], dst.at[rows(a, tokens), cols(0, width, base)])


def to_tokens(src, dst, tokens, width):
    return lambda a, b: (src.at[rows(b, tokens), :], dst.at[:, cols(a, width)])


def kernel_in(n, heads, key, value, ids, pair, ids_all, send, recv, local, isend, irecv):
    s = lax.axis_index("seq")
    tokens, width = key.shape[0], key.shape[1] // heads
    greet(n, heads)
    copies, own = exchange(
        [to_heads(key, pair, tokens, width), to_heads(value, pair, tokens, width, width)],
        heads, send, recv, local,
    )

    def idc(d):
        return pltpu.make_async_remote_copy(
            src_ref=ids, dst_ref=ids_all.at[s], send_sem=isend.at[d], recv_sem=irecv.at[d],
            device_id={"seq": lax.rem(s + d, n)}, device_id_type=MESH,
        )

    mine = pltpu.make_async_copy(ids, ids_all.at[s], local.at[2])
    for c in copies:
        c.start()
    each(n, lambda d: idc(d).start())
    mine.start()
    for c in own:
        c.start()
    each(n, lambda d: idc(d).wait())
    mine.wait()
    for c in own:
        c.wait()
    for c in copies:
        c.wait()


def spread(n, src_of, dst, send, recv):
    s = lax.axis_index("seq")

    def make(d):
        peer = lax.rem(s + d, n)
        return pltpu.make_async_remote_copy(
            src_ref=src_of(peer), dst_ref=dst.at[s], send_sem=send.at[d], recv_sem=recv.at[d],
            device_id={"seq": peer}, device_id_type=MESH,
        )

    return make


def halo(n, low, high, got, send, recv):
    s = lax.axis_index("seq")
    out = []
    for k, (src, step) in enumerate(((high, 1), (low, n - 1))):
        out.append(
            pltpu.make_async_remote_copy(
                src_ref=src, dst_ref=got.at[k], send_sem=send.at[k], recv_sem=recv.at[k],
                device_id={"seq": lax.rem(s + step, n)}, device_id_type=MESH,
            )
        )
    return out


def traffic(n, heads, views, block_src, block_dst, low, high, halos, gsrc, ghere, gmine, gall,
            combine, sems):
    s = lax.axis_index("seq")
    send, recv, local, bs, br, hs, hr, gs, gr, fs, fr = sems
    greet(n, heads)
    first = spread(n, lambda p: gsrc.at[p], ghere, gs, gr)
    blocks = spread(n, lambda p: block_src.at[p], block_dst, bs, br)
    final = spread(n, lambda p: gmine, gall, fs, fr)
    edges = halo(n, low, high, halos, hs, hr)
    copies, own = exchange(views, heads, send, recv, local)
    own.append(pltpu.make_async_copy(block_src.at[s], block_dst.at[s], local.at[len(views)]))
    keep = pltpu.make_async_copy(gsrc.at[s], ghere.at[s], local.at[len(views) + 1])
    each(n, lambda d: first(d).start())
    keep.start()
    each(n, lambda d: blocks(d).start())
    for c in copies + edges + own:
        c.start()
    keep.wait()
    each(n, lambda d: first(d).wait())
    total = combine(ghere)
    gmine[...] = total
    gall[s] = total
    each(n, lambda d: final(d).start())
    for c in copies + edges + own:
        c.wait()
    each(n, lambda d: final(d).wait())
    each(n, lambda d: blocks(d).wait())


def kernel_fetch(n, heads, owners, query, grad, outgoing, pair, gcon,
                 qh, gh, incoming, halos, gall, ghere, gmine, *sems):
    tokens, width = query.shape[0], query.shape[1] // heads
    last = pair.shape[0] - BLOCK
    slot = lax.axis_index("seq") * GLOBALS // n
    traffic(
        n, heads, [to_heads(query, qh, tokens, width), to_heads(grad, gh, tokens, width)],
        outgoing, incoming, pair.at[pl.ds(0, BLOCK)], pair.at[pl.ds(last, BLOCK)], halos,
        gcon, ghere, gmine, gall, lambda ref: ref[owners[slot]], sems,
    )


def kernel_return(n, heads, att, qg, sending, edge, gsend,
                  out, qout, returned, halos, gall, ghere, gmine, *sems):
    width = att.shape[1]
    tokens = att.shape[0] // heads

    def combine(ref):
        def add(i, acc):
            return acc + ref[i].astype(jnp.float32)

        zero = jnp.zeros(ref.shape[1:], jnp.float32)
        return lax.fori_loop(0, n, add, zero).astype(jnp.bfloat16)

    traffic(
        n, heads, [to_tokens(att, out, tokens, width), to_tokens(qg, qout, tokens, width)],
        sending, returned, edge.at[0], edge.at[1], halos, gsend, ghere, gmine, gall, combine, sems,
    )


def kernel_out(heads, kg, vg, kout, vout, send, recv, local):
    width = kg.shape[1]
    tokens = kg.shape[0] // heads
    greet(0, heads)
    copies, own = exchange(
        [to_tokens(kg, kout, tokens, width), to_tokens(vg, vout, tokens, width)],
        heads, send, recv, local,
    )
    for c in copies + own:
        c.start()
    for c in own + copies:
        c.wait()


def dot(a, b, ca, cb):
    return lax.dot_general(a, b, (((ca,), (cb,)), ((), ())), preferred_element_type=jnp.float32)


def kernel_attend(n, lanes, slots, qh, gh, pair, halos, incoming, gall,
                  att, qg, wsum, edge, sending, gsum, pairs, keys, gacc):
    nb = qh.shape[0] // BLOCK
    width = qh.shape[1]
    s = lax.axis_index("seq")
    per = lanes // HEAD_DIM
    scale = HEAD_DIM ** (-0.5)
    pairs[pl.ds(0, BLOCK)] = halos[0]
    pairs[pl.ds(BLOCK, nb * BLOCK)] = pair[...]
    pairs[pl.ds((nb + 1) * BLOCK, BLOCK)] = halos[1]
    keys[pl.ds((3 + RANDOM) * BLOCK, GLOBALS * BLOCK)] = gall[...]
    gacc[...] = jnp.zeros_like(gacc)
    wsum[...] = jnp.zeros_like(wsum)
    if n > RANDOM * nb:
        sending[...] = jnp.zeros_like(sending)
    lane_head = lax.broadcasted_iota(jnp.int32, (BLOCK, lanes), 1) // HEAD_DIM
    part = lax.broadcasted_iota(jnp.int32, (1, PARTS * BLOCK), 1) // BLOCK

    def stack(x):
        zero = jnp.zeros_like(x)
        return jnp.concatenate([jnp.where(lane_head == j, x, zero) for j in range(per)], axis=0)

    def unstack(x):
        got = x[0:BLOCK]
        for j in range(1, per):
            got = jnp.where(lane_head == j, x[j * BLOCK : (j + 1) * BLOCK], got)
        return got

    def block(b, carry):
        here = pl.ds(pl.multiple_of(b * BLOCK, BLOCK), BLOCK)
        window = pl.ds(pl.multiple_of(b * BLOCK, BLOCK), 3 * BLOCK)
        keys[pl.ds(0, 3 * BLOCK)] = pairs[window]
        for r in range(RANDOM):
            keys[pl.ds((3 + r) * BLOCK, BLOCK)] = incoming[slots[b * RANDOM + r]]
        number = s * nb + b
        bad = ((part == 0) & (number == 0)) | ((part == 2) & (number == n * nb - 1))
        for g in range(width // lanes):
            at = pl.ds(g * lanes, lanes)
            vat = pl.ds(width + g * lanes, lanes)
            q = stack(qh[here, at])
            do = stack(gh[here, at])
            k = keys[:, at]
            v = keys[:, vat]
            scores = jnp.where(bad, MASKED, dot(q, k, 1, 1) * scale)
            raw = jnp.exp(scores - jnp.max(scores, axis=-1, keepdims=True))
            probs = raw * (1.0 / jnp.sum(raw, axis=-1, keepdims=True))
            half = probs.astype(jnp.bfloat16)
            attended = dot(half, v, 1, 0)
            delta = jnp.sum(do.astype(jnp.float32) * attended, axis=-1, keepdims=True)
            ds = (probs * (dot(do, v, 1, 1) - delta)).astype(jnp.bfloat16)
            att[here, at] = unstack(attended).astype(jnp.bfloat16)
            qg[here, at] = (unstack(dot(ds, k, 1, 0)) * scale).astype(jnp.bfloat16)
            for x, y, to, mult in ((ds, q, at, scale), (half, do, vat, 1.0)):
                grad = dot(x, y, 0, 0) * mult
                wsum[window, to] += grad[: 3 * BLOCK]
                for r in range(RANDOM):
                    low = (3 + r) * BLOCK
                    sending[slots[b * RANDOM + r], :, to] = grad[low : low + BLOCK].astype(
                        jnp.bfloat16
                    )
                gacc[:, to] += grad[(3 + RANDOM) * BLOCK :]
        return carry

    lax.fori_loop(0, nb, block, 0)
    edge[0] = wsum[pl.ds(0, BLOCK)].astype(jnp.bfloat16)
    edge[1] = wsum[pl.ds((nb + 1) * BLOCK, BLOCK)].astype(jnp.bfloat16)
    gsum[...] = gacc[...].astype(jnp.bfloat16)


def kernel_sum(n, served, owners, owned_at, wsum, halos, returned, gall, kg, vg, acc):
    nb = kg.shape[0] // BLOCK
    width = kg.shape[1]
    s = lax.axis_index("seq")
    acc[...] = wsum[pl.ds(BLOCK, nb * BLOCK)]
    acc[pl.ds(0, BLOCK)] += halos[0].astype(jnp.float32)
    acc[pl.ds((nb - 1) * BLOCK, BLOCK)] += halos[1].astype(jnp.float32)

    def add(i, c):
        at = pl.ds(pl.multiple_of(served[i] * BLOCK, BLOCK), BLOCK)
        acc[at] += returned[i].astype(jnp.float32)
        return c

    lax.fori_loop(0, n, add, 0)
    for g in range(GLOBALS):

        @pl.when(owners[g] == s)
        def _():
            at = pl.ds(pl.multiple_of(owned_at[g] * BLOCK, BLOCK), BLOCK)
            acc[at] += gall[pl.ds(g * BLOCK, BLOCK)].astype(jnp.float32)

    kg[...] = acc[:, pl.ds(0, width)].astype(jnp.bfloat16)
    vg[...] = acc[:, pl.ds(width, width)].astype(jnp.bfloat16)


def body(n, heads, query_rows, key_rows, value_rows, out_grad, random_blocks, global_blocks):
    bf = jnp.bfloat16
    tokens, full = query_rows.shape
    width = full // heads
    total = tokens * heads
    nb = total // BLOCK
    me = lax.axis_index("seq")
    dma = pltpu.SemaphoreType.DMA
    sds = jax.ShapeDtypeStruct
    requests = RANDOM * nb
    flat = random_blocks.reshape(requests)
    ids = jnp.broadcast_to(jnp.pad(flat, (0, 128 - requests))[None], (8, 128))
    pair, ids_all = pl.pallas_call(
        partial(kernel_in, n, heads),
        out_shape=(sds((total, 2 * width), bf), sds((n, 8, 128), jnp.int32)),
        in_specs=[VMEM] * 3,
        out_specs=(VMEM,) * 2,
        scratch_shapes=[dma((2 * heads,)), dma((2 * heads,)), dma((3,)), dma((n,)), dma((n,))],
        compiler_params=params(0),
        name="head_in",
    )(key_rows, value_rows, ids)
    asked = ids_all[:, 0, :requests]
    served = jnp.sum(jnp.where(asked // nb == me, asked % nb, 0), axis=1).astype(jnp.int32)
    owners = global_blocks // nb
    owned_at = global_blocks % nb
    pair_blocks = pair.reshape(nb, BLOCK, 2 * width)
    outgoing = jnp.take(pair_blocks, served, axis=0, mode="clip")
    chunk = GLOBALS * BLOCK // n
    gcon = jnp.take(pair_blocks, owned_at, axis=0, mode="clip").reshape(n, chunk, 2 * width)
    slab = sds((n, BLOCK, 2 * width), bf)
    small = sds((n, chunk, 2 * width), bf)
    sems = [dma((2 * heads,)), dma((2 * heads,)), dma((4,)), dma((n,)), dma((n,)),
            dma((2,)), dma((2,)), dma((n,)), dma((n,)), dma((n,)), dma((n,))]
    scratch = [pltpu.VMEM(small.shape, bf), pltpu.VMEM(small.shape[1:], bf)] + sems
    edges = sds((2, BLOCK, 2 * width), bf)
    qh, gh, incoming, halos, gall = pl.pallas_call(
        partial(kernel_fetch, n, heads),
        out_shape=(sds((total, width), bf), sds((total, width), bf), slab, edges, small),
        in_specs=[SMEM] + [VMEM] * 5,
        out_specs=(VMEM,) * 5,
        scratch_shapes=scratch,
        compiler_params=params(1),
        name="fetch",
    )(owners, query_rows, out_grad, outgoing, pair, gcon)
    gwide = (GLOBALS * BLOCK, 2 * width)
    att, qg, wsum, edge, sending, gsum = pl.pallas_call(
        partial(kernel_attend, n, min(256, width)),
        out_shape=(
            sds((total, width), bf), sds((total, width), bf),
            sds(((nb + 2) * BLOCK, 2 * width), jnp.float32), edges, slab, sds(gwide, bf),
        ),
        in_specs=[SMEM] + [VMEM] * 6,
        out_specs=(VMEM,) * 6,
        scratch_shapes=[
            pltpu.VMEM(((nb + 2) * BLOCK, 2 * width), bf),
            pltpu.VMEM((PARTS * BLOCK, 2 * width), bf),
            pltpu.VMEM(gwide, jnp.float32),
        ],
        compiler_params=pltpu.CompilerParams(vmem_limit_bytes=48 * 1024 * 1024),
        name="attend",
    )(flat // nb, qh, gh, pair, halos, incoming, gall.reshape(gwide))
    out, qout, returned, back, gtot = pl.pallas_call(
        partial(kernel_return, n, heads),
        out_shape=(sds((tokens, full), bf), sds((tokens, full), bf), slab, edges, small),
        in_specs=[VMEM] * 5,
        out_specs=(VMEM,) * 5,
        scratch_shapes=scratch,
        compiler_params=params(2),
        name="give_back",
    )(att, qg, sending, edge, gsum.reshape(n, chunk, 2 * width))
    kg, vg = pl.pallas_call(
        partial(kernel_sum, n),
        out_shape=(sds((total, width), bf),) * 2,
        in_specs=[SMEM] * 3 + [VMEM] * 4,
        out_specs=(VMEM,) * 2,
        scratch_shapes=[pltpu.VMEM((total, 2 * width), jnp.float32)],
        compiler_params=pltpu.CompilerParams(vmem_limit_bytes=48 * 1024 * 1024),
        name="sum_owned",
    )(served, owners, owned_at, wsum, back, returned, gtot.reshape(gwide))
    kout, vout = pl.pallas_call(
        partial(kernel_out, heads),
        out_shape=(sds((tokens, full), bf),) * 2,
        in_specs=[VMEM] * 2,
        out_specs=(VMEM,) * 2,
        scratch_shapes=[dma((2 * heads,)), dma((2 * heads,)), dma((2,))],
        compiler_params=params(3),
        name="head_out",
    )(kg, vg)
    return out, qout, kout, vout


def solution(mesh):
    rows_spec = P(("seq", "head"), None)
    return jax.shard_map(
        partial(body, mesh.shape["seq"], mesh.shape["head"]),
        mesh=mesh,
        in_specs=(rows_spec,) * 4 + (P("seq", None), P()),
        out_specs=(rows_spec,) * 4,
        check_vma=False,
    )
```

time: 471 us -> 195 us (0.41)
  Pallas kernels: 0 us -> 183 us
  waiting for transfers between devices: 122 us -> 0 us
  local copies, waits for them, and re-layouts: 125 us -> 10 us
  blocking collectives: 93.7 us -> 0 us
  starting transfers between devices: 49.9 us -> 0 us
  other arithmetic: 34 us -> 0.82 us
  matrix products: 27.1 us -> 0 us
  between operations: 15.9 us -> 0.74 us
    pallas_call x0 -> x6, Pallas kernels: none -> 183 us  [the longest x1 64 us: body(): pl.pallas_call(partial(kernel_return, n, heads), out_shape=(sds((tokens,...]
    psum x1 -> x0, waiting for transfers between devices: 84.8 us -> none  [body(): global_total = lax.psum(jnp.sum(global_grad, axis=0), 'seq')]
    psum x1 -> x0, blocking collectives: 84.3 us -> none  [body(): lax.psum(jnp.where(held, pieces, 0.0), 'seq').astype(jnp.bfloat16)]
    concatenate x5 -> x0, local copies, waits for them, and re-layouts: 52.3 us -> none  [the longest x4 50.6 us: attend_group(): jnp.concatenate([key_grad.reshape(groups, key_count, width_here), value_g...]
    all_to_all x10 -> x0, starting transfers between devices: 40.7 us -> none  [the longest x1 7.39 us: body(): lax.all_to_all(asked_for, 'seq', split_axis=0, concat_axis=0, tiled=True)]
    all_to_all x10 -> x0, waiting for transfers between devices: 37.5 us -> none  [the longest x1 7.06 us: body(): lax.all_to_all(query_grad, 'head', split_axis=0, concat_axis=1, tiled=True)]
    slice x7 -> x1, local copies, waits for them, and re-layouts: 24.1 us -> 0.01 us  [body(): asked = ids_all[:, 0, :requests]]
    dot_general x6 -> x0, matrix products: 18.6 us -> none  [the longest x1 4.5 us: attend_group(): jnp.einsum('ghqk,gqhd->gkhd', probs_half, grad_heads, preferred_element_t...]
  transfers between devices with their start and end apart: 15 -> 0, of which waited for: 9 -> 0; matrix products, arithmetic and copies ran while one was open for 14% -> 0% of each run, Pallas kernels for 0% -> 0%
where the time goes in v1:
time: 195 us
  Pallas kernels  183 us (94%)
  local copies, waits for them, and re-layouts  10 us (5%)
    pallas_call x1, Pallas kernels, body(): pl.pallas_call(partial(kernel_return, n, heads), out_shape=(sds((tokens,...  64 us
    pallas_call x1, Pallas kernels, body(): pl.pallas_call(partial(kernel_fetch, n, heads), out_shape=(sds((total, wi...  63.4 us
    pallas_call x1, Pallas kernels, body(): pl.pallas_call(partial(kernel_in, n, heads), out_shape=(sds((total, 2 * w...  20.1 us
    pallas_call x1, Pallas kernels, body(): pl.pallas_call(partial(kernel_attend, n, min(256, width)), out_shape=(sds...  19.4 us
    pallas_call x1, Pallas kernels, body(): pl.pallas_call(partial(kernel_out, heads), out_shape=(sds((tokens, full),...  14 us
    unnamed x15, local copies, waits for them, and re-layouts  7.35 us

profile of v1, /device:TPU:0, one launch (start us, length us, event | category | flops | bytes accessed | tf_op | source)
XLA Modules:
  0.0 195.1 jit_solution(11363179405715755512)
XLA Ops:
  0.6 0.7 and_select_fusion
  1.3 0.8 copy.11
  2.1 0.1 reshape.27
  2.2 0.0 copy-start.3
  2.2 1.0 copy-done.3
  3.2 0.0 copy-start.4
  3.2 1.0 copy-done.4
  4.3 20.1 %head_in.1 = (bf16[512,1024]{1,0:T(8,128)(2,1)S(1)}, s32[16,8,128]{2,1,0:T(8,128)S(1)}) custom-call(bf16[256,1024]{1,0:T(8,128)(2,1)S(1)} %copy-done.3, bf16[256,1024]{1,0:T(8,128)(2,1)S(1)} %copy-done.4, s32[8,128]{1,0:T(8,128)S(1)} %broadcast_in_dim.16.ids), custom_call_target="tpu_custom_call" | custom-call | tf_op jit(solution)/shard_map/head_in/pallas_call | solution.py:332
  24.4 0.1 fusion.2.served
  24.5 0.6 gather_fusion.1
  25.1 0.0 copy-start.1
  25.1 0.0 copy-start.2
  25.1 2.0 %gather_fusion = bf16[16,64,1024]{2,1,0:T(8,128)(2,1)} fusion(bf16[8,64,1024]{2,1,0:T(8,128)(2,1)S(1)} %bitcast.7, s32[1024]{0:T(1024)S(1)} %pad_clamp_fusion.1), kind=kCustom, calls=%fused_computation | custom fusion | bytes 4194368 | tf_op jit(solution)/shard_map/jit(_take)/gather | solution.py:346
  27.1 0.0 copy-done.1
  27.1 0.0 copy-done.2
  27.2 63.4 %fetch.1 = (bf16[512,512]{1,0:T(8,128)(2,1)S(1)}, bf16[512,512]{1,0:T(8,128)(2,1)S(1)}, bf16[16,64,1024]{2,1,0:T(8,128)(2,1)S(1)}, bf16[2,64,1024]{2,1,0:T(8,128)(2,1)S(1)}, bf16[16,8,1024]{2,1,0:T(8,128)(2,1)S(1)}) custom-call(s32[2]{0:T(128)S(1)} %get-tuple-element.49.owners, bf16[256,1024]{1,0:T(8,128)(2,1)S(1)} %copy-done.1, ...), custom_call_target="tpu_custom_call" | custom-call | tf_op jit(solution)/shard_map/fetch/pallas_call | solution.py:355
  90.6 0.0 copy-start
  90.6 1.3 copy-done
  91.9 19.4 %attend.1 = (bf16[512,512]{1,0:T(8,128)(2,1)S(1)}, bf16[512,512]{1,0:T(8,128)(2,1)S(1)}, f32[640,1024]{1,0:T(8,128)}, bf16[2,64,1024]{2,1,0:T(8,128)(2,1)S(1)}, ...) custom-call(s32[16]{0:T(128)S(1)} %and_select_fusion.2.slots, bf16[512,512]{1,0:T(8,128)(2,1)S(1)} %get-tuple-element.28.qh, ...), custom_call_target="tpu_custom_call" | custom-call | tf_op jit(solution)/shard_map/attend/pallas_call | solution.py:365
  111.4 64.0 %give_back.1 = (bf16[256,1024]{1,0:T(8,128)(2,1)S(1)}, bf16[256,1024]{1,0:T(8,128)(2,1)S(1)}, bf16[16,64,1024]{2,1,0:T(8,128)(2,1)S(1)}, bf16[2,64,1024]{2,1,0:T(8,128)(2,1)S(1)}, bf16[16,8,1024]{2,1,0:T(8,128)(2,1)S(1)}) custom-call(bf16[512,512]{1,0:T(8,128)(2,1)S(1)} %get-tuple-element.33.att, bf16[512,512]{1,0:T(8,128)(2,1)S(1)} %get-tuple-element.34.qg, ...), custom_call_target="tpu_custom_call" | custom-call | tf_op jit(solution)/shard_map/give_back/pallas_call | solution.py:381
  175.4 2.5 %sum_owned.1 = (bf16[512,512]{1,0:T(8,128)(2,1)S(1)}, bf16[512,512]{1,0:T(8,128)(2,1)S(1)}) custom-call(s32[16]{0:T(128)S(1)} %fusion.2.served, s32[2]{0:T(128)S(1)} %get-tuple-element.49.owners, s32[2]{0:T(128)S(1)} %get-tuple-element.48.owned_at, f32[640,1024]{1,0:T(8,128)} %get-tuple-element.40.wsum, bf16[2,64,1024]{2,1,0:T(8,128)(2,1)S(1)} %get-tuple-element.41.halos, ...), custom_call_target="tpu_custom_call" | custom-call | tf_op jit(solution)/shard_map/sum_owned/pallas_call | solution.py:390
  177.8 14.0 %head_out.1 = (bf16[256,1024]{1,0:T(8,128)(2,1)S(1)}, bf16[256,1024]{1,0:T(8,128)(2,1)S(1)}) custom-call(bf16[512,512]{1,0:T(8,128)(2,1)S(1)} %get-tuple-element.44.kg, bf16[512,512]{1,0:T(8,128)(2,1)S(1)} %get-tuple-element.45.vg), custom_call_target="tpu_custom_call" | custom-call | tf_op jit(solution)/shard_map/head_out/pallas_call | solution.py:399
  191.9 0.8 copy.16
  192.7 0.8 copy.17
  193.5 0.8 copy.18
  194.3 0.8 copy.19
  (6 shorter events, 0.0 us)
Async XLA Ops:
  2.2 1.0 copy-start.3
  3.2 1.0 copy-start.4
  25.1 2.0 %copy-start.1 = (bf16[256,1024]{1,0:T(8,128)(2,1)S(1)}, bf16[256,1024]{1,0:T(8,128)(2,1)}, u32[]{:S(2)}) copy-start(bf16[256,1024]{1,0:T(8,128)(2,1)} %query.1) | copy-start | bytes 1572868
  25.1 2.0 %copy-start.2 = (bf16[256,1024]{1,0:T(8,128)(2,1)S(1)}, bf16[256,1024]{1,0:T(8,128)(2,1)}, u32[]{:S(2)}) copy-start(bf16[256,1024]{1,0:T(8,128)(2,1)} %grad.1) | copy-start | bytes 1572868
  90.6 1.3 copy-start

commit v2 on v1

--- a/solution.py
+++ b/solution.py
@@ -15,6 +15,7 @@
 MASKED = -1e30
 MESH = pl.DeviceIdType.MESH
 VMEM = pl.BlockSpec(memory_space=pltpu.VMEM)
+ANY = pl.BlockSpec(memory_space=pl.ANY)
 SMEM = pl.BlockSpec(memory_space=pltpu.SMEM)
 
 
@@ -146,49 +147,90 @@
     return out
 
 
-def traffic(n, heads, views, block_src, block_dst, low, high, halos, gsrc, ghere, gmine, gall,
-            combine, sems):
-    s = lax.axis_index("seq")
-    send, recv, local, bs, br, hs, hr, gs, gr, fs, fr = sems
+def traffic(n, heads, views, block_src, block_dst, low, high, halos, gsrc, ghere, gmine, glayer,
+            gdone, gall, first, second, sems):
+    s = lax.axis_index("seq")
+    send, recv, local, bs, br, hs, hr, gs, gr, ls, lr, fs, fr = sems
+    group = gsrc.shape[0]
+    layers = n // group
+    mine, layer = lax.rem(s, group), s // group
     greet(n, heads)
-    first = spread(n, lambda p: gsrc.at[p], ghere, gs, gr)
     blocks = spread(n, lambda p: block_src.at[p], block_dst, bs, br)
-    final = spread(n, lambda p: gmine, gall, fs, fr)
     edges = halo(n, low, high, halos, hs, hr)
     copies, own = exchange(views, heads, send, recv, local)
     own.append(pltpu.make_async_copy(block_src.at[s], block_dst.at[s], local.at[len(views)]))
-    keep = pltpu.make_async_copy(gsrc.at[s], ghere.at[s], local.at[len(views) + 1])
-    each(n, lambda d: first(d).start())
-    keep.start()
-    each(n, lambda d: blocks(d).start())
+    keep = pltpu.make_async_copy(gsrc.at[mine], ghere.at[mine], local.at[len(views) + 1])
+
+    def inside(src_of, dst, ss, rs):
+        out = []
+        for j in range(1, group):
+            to = lax.rem(mine + j, group)
+            out.append(
+                pltpu.make_async_remote_copy(
+                    src_ref=src_of(to), dst_ref=dst.at[mine], send_sem=ss.at[j],
+                    recv_sem=rs.at[j], device_id={"seq": layer * group + to},
+                    device_id_type=MESH,
+                )
+            )
+        return out
+
+    def across(j):
+        return pltpu.make_async_remote_copy(
+            src_ref=gmine, dst_ref=glayer.at[layer], send_sem=ls.at[j], recv_sem=lr.at[j],
+            device_id={"seq": lax.rem(layer + j, layers) * group + mine}, device_id_type=MESH,
+        )
+
+    def distance(i):
+        return n // 2 + ((i + 1) // 2) * (2 * lax.rem(i, 2) - 1)
+
+    def go(i, c):
+        blocks(distance(i)).start()
+        return c
+
+    step1 = inside(lambda to: gsrc.at[to], ghere, gs, gr)
+    step3 = inside(lambda to: gdone, gall, fs, fr)
+    for c in step1 + [keep]:
+        c.start()
+    lax.fori_loop(0, n // 2, go, 0)
     for c in copies + edges + own:
         c.start()
-    keep.wait()
-    each(n, lambda d: first(d).wait())
-    total = combine(ghere)
-    gmine[...] = total
-    gall[s] = total
-    each(n, lambda d: final(d).start())
+    for c in step1 + [keep]:
+        c.wait()
+    part = first(ghere)
+    gmine[...] = part
+    glayer[layer] = part
+    each(layers, lambda j: across(j).start())
+    lax.fori_loop(n // 2, n - 1, go, 0)
     for c in copies + edges + own:
         c.wait()
-    each(n, lambda d: final(d).wait())
+    each(layers, lambda j: across(j).wait())
+    total = second(glayer)
+    gdone[...] = total
+    gall[mine] = total
+    for c in step3:
+        c.start()
+    for c in step3:
+        c.wait()
     each(n, lambda d: blocks(d).wait())
 
 
 def kernel_fetch(n, heads, owners, query, grad, outgoing, pair, gcon,
-                 qh, gh, incoming, halos, gall, ghere, gmine, *sems):
+                 qh, gh, incoming, halos, gall, ghere, gmine, glayer, gdone, *sems):
     tokens, width = query.shape[0], query.shape[1] // heads
     last = pair.shape[0] - BLOCK
-    slot = lax.axis_index("seq") * GLOBALS // n
+    group = gcon.shape[0]
+    slot = lax.rem(lax.axis_index("seq"), group) * GLOBALS // group
     traffic(
         n, heads, [to_heads(query, qh, tokens, width), to_heads(grad, gh, tokens, width)],
         outgoing, incoming, pair.at[pl.ds(0, BLOCK)], pair.at[pl.ds(last, BLOCK)], halos,
-        gcon, ghere, gmine, gall, lambda ref: ref[owners[slot]], sems,
+        gcon, ghere, gmine, glayer, gdone, gall,
+        lambda ref: ref[lax.rem(owners[slot], group)], lambda ref: ref[owners[slot] // group],
+        sems,
     )
 
 
 def kernel_return(n, heads, att, qg, sending, edge, gsend,
-                  out, qout, returned, halos, gall, ghere, gmine, *sems):
+                  out, qout, returned, halos, gall, ghere, gmine, glayer, gdone, *sems):
     width = att.shape[1]
     tokens = att.shape[0] // heads
 
@@ -197,11 +239,12 @@
             return acc + ref[i].astype(jnp.float32)
 
         zero = jnp.zeros(ref.shape[1:], jnp.float32)
-        return lax.fori_loop(0, n, add, zero).astype(jnp.bfloat16)
+        return lax.fori_loop(0, ref.shape[0], add, zero).astype(jnp.bfloat16)
 
     traffic(
         n, heads, [to_tokens(att, out, tokens, width), to_tokens(qg, qout, tokens, width)],
-        sending, returned, edge.at[0], edge.at[1], halos, gsend, ghere, gmine, gall, combine, sems,
+        sending, returned, edge.at[0], edge.at[1], halos, gsend, ghere, gmine, glayer, gdone,
+        gall, combine, combine, sems,
     )
 
 
@@ -229,7 +272,7 @@
     width = qh.shape[1]
     s = lax.axis_index("seq")
     per = lanes // HEAD_DIM
-    scale = HEAD_DIM ** (-0.5)
+    scale = jnp.asarray(HEAD_DIM ** (-0.5), jnp.bfloat16)
     pairs[pl.ds(0, BLOCK)] = halos[0]
     pairs[pl.ds(BLOCK, nb * BLOCK)] = pair[...]
     pairs[pl.ds((nb + 1) * BLOCK, BLOCK)] = halos[1]
@@ -239,7 +282,7 @@
     if n > RANDOM * nb:
         sending[...] = jnp.zeros_like(sending)
     lane_head = lax.broadcasted_iota(jnp.int32, (BLOCK, lanes), 1) // HEAD_DIM
-    part = lax.broadcasted_iota(jnp.int32, (1, PARTS * BLOCK), 1) // BLOCK
+    part = lax.broadcasted_iota(jnp.int32, (PARTS * BLOCK, 1), 0) // BLOCK
 
     def stack(x):
         zero = jnp.zeros_like(x)
@@ -262,21 +305,21 @@
         for g in range(width // lanes):
             at = pl.ds(g * lanes, lanes)
             vat = pl.ds(width + g * lanes, lanes)
-            q = stack(qh[here, at])
+            q = stack(qh[here, at]) * scale
             do = stack(gh[here, at])
             k = keys[:, at]
             v = keys[:, vat]
-            scores = jnp.where(bad, MASKED, dot(q, k, 1, 1) * scale)
-            raw = jnp.exp(scores - jnp.max(scores, axis=-1, keepdims=True))
-            probs = raw * (1.0 / jnp.sum(raw, axis=-1, keepdims=True))
+            scores = jnp.where(bad, MASKED, dot(k, q, 1, 1))
+            raw = jnp.exp(scores - jnp.max(scores, axis=0, keepdims=True))
+            probs = raw * (1.0 / jnp.sum(raw, axis=0, keepdims=True))
             half = probs.astype(jnp.bfloat16)
-            attended = dot(half, v, 1, 0)
-            delta = jnp.sum(do.astype(jnp.float32) * attended, axis=-1, keepdims=True)
-            ds = (probs * (dot(do, v, 1, 1) - delta)).astype(jnp.bfloat16)
-            att[here, at] = unstack(attended).astype(jnp.bfloat16)
-            qg[here, at] = (unstack(dot(ds, k, 1, 0)) * scale).astype(jnp.bfloat16)
-            for x, y, to, mult in ((ds, q, at, scale), (half, do, vat, 1.0)):
-                grad = dot(x, y, 0, 0) * mult
+            pgrad = dot(v, do, 1, 1)
+            delta = jnp.sum(half.astype(jnp.float32) * pgrad, axis=0, keepdims=True)
+            ds = (probs * (pgrad - delta)).astype(jnp.bfloat16)
+            att[here, at] = unstack(dot(half, v, 0, 0)).astype(jnp.bfloat16)
+            qg[here, at] = (unstack(dot(ds, k, 0, 0)) * HEAD_DIM ** (-0.5)).astype(jnp.bfloat16)
+            for x, y, to in ((ds, q, at), (half, do, vat)):
+                grad = dot(x, y, 1, 0)
                 wsum[window, to] += grad[: 3 * BLOCK]
                 for r in range(RANDOM):
                     low = (3 + r) * BLOCK
@@ -332,7 +375,7 @@
     pair, ids_all = pl.pallas_call(
         partial(kernel_in, n, heads),
         out_shape=(sds((total, 2 * width), bf), sds((n, 8, 128), jnp.int32)),
-        in_specs=[VMEM] * 3,
+        in_specs=[ANY, ANY, VMEM],
         out_specs=(VMEM,) * 2,
         scratch_shapes=[dma((2 * heads,)), dma((2 * heads,)), dma((3,)), dma((n,)), dma((n,))],
         compiler_params=params(0),
@@ -344,18 +387,23 @@
     owned_at = global_blocks % nb
     pair_blocks = pair.reshape(nb, BLOCK, 2 * width)
     outgoing = jnp.take(pair_blocks, served, axis=0, mode="clip")
-    chunk = GLOBALS * BLOCK // n
-    gcon = jnp.take(pair_blocks, owned_at, axis=0, mode="clip").reshape(n, chunk, 2 * width)
+    group = 4
+    layers = n // group
+    chunk = GLOBALS * BLOCK // group
+    gcon = jnp.take(pair_blocks, owned_at, axis=0, mode="clip").reshape(group, chunk, 2 * width)
     slab = sds((n, BLOCK, 2 * width), bf)
-    small = sds((n, chunk, 2 * width), bf)
+    small = sds((group, chunk, 2 * width), bf)
     sems = [dma((2 * heads,)), dma((2 * heads,)), dma((4,)), dma((n,)), dma((n,)),
-            dma((2,)), dma((2,)), dma((n,)), dma((n,)), dma((n,)), dma((n,))]
-    scratch = [pltpu.VMEM(small.shape, bf), pltpu.VMEM(small.shape[1:], bf)] + sems
+            dma((2,)), dma((2,)), dma((group,)), dma((group,)), dma((layers,)), dma((layers,)),
+            dma((group,)), dma((group,))]
+    wide = (chunk, 2 * width)
+    scratch = [pltpu.VMEM(small.shape, bf), pltpu.VMEM(wide, bf),
+               pltpu.VMEM((layers,) + wide, bf), pltpu.VMEM(wide, bf)] + sems
     edges = sds((2, BLOCK, 2 * width), bf)
     qh, gh, incoming, halos, gall = pl.pallas_call(
         partial(kernel_fetch, n, heads),
         out_shape=(sds((total, width), bf), sds((total, width), bf), slab, edges, small),
-        in_specs=[SMEM] + [VMEM] * 5,
+        in_specs=[SMEM, ANY, ANY] + [VMEM] * 3,
         out_specs=(VMEM,) * 5,
         scratch_shapes=scratch,
         compiler_params=params(1),
@@ -386,7 +434,7 @@
         scratch_shapes=scratch,
         compiler_params=params(2),
         name="give_back",
-    )(att, qg, sending, edge, gsum.reshape(n, chunk, 2 * width))
+    )(att, qg, sending, edge, gsum.reshape(group, chunk, 2 * width))
     kg, vg = pl.pallas_call(
         partial(kernel_sum, n),
         out_shape=(sds((total, width), bf),) * 2,

time: 195 us -> 186 us (0.954)
  Pallas kernels: 183 us -> 174 us
    pallas_call x1, Pallas kernels: 64 us -> 60.5 us  [body(): pl.pallas_call(partial(kernel_return, n, heads), out_shape=(sds((tokens,...]
    pallas_call x1, Pallas kernels: 63.4 us -> 60 us  [body(): pl.pallas_call(partial(kernel_fetch, n, heads), out_shape=(sds((total, wi...]
    pallas_call x1, Pallas kernels: 19.4 us -> 16.9 us  [body(): pl.pallas_call(partial(kernel_attend, n, min(256, width)), out_shape=(sds...]
where the time goes in v2:
time: 186 us
  Pallas kernels  174 us (94%)
  local copies, waits for them, and re-layouts  10 us (5%)
    pallas_call x1, Pallas kernels, body(): pl.pallas_call(partial(kernel_return, n, heads), out_shape=(sds((tokens,...  60.5 us
    pallas_call x1, Pallas kernels, body(): pl.pallas_call(partial(kernel_fetch, n, heads), out_shape=(sds((total, wi...  60 us
    pallas_call x1, Pallas kernels, body(): pl.pallas_call(partial(kernel_in, n, heads), out_shape=(sds((total, 2 * w...  20.1 us
    pallas_call x1, Pallas kernels, body(): pl.pallas_call(partial(kernel_attend, n, min(256, width)), out_shape=(sds...  16.9 us
    pallas_call x1, Pallas kernels, body(): pl.pallas_call(partial(kernel_out, heads), out_shape=(sds((tokens, full),...  14.5 us
    unnamed x15, local copies, waits for them, and re-layouts  7.35 us

profile of v2, /device:TPU:0, one launch (start us, length us, event | category | flops | bytes accessed | tf_op | source)
XLA Modules:
  0.0 185.9 jit_solution(1106977863664869517)
XLA Ops:
  0.6 0.7 and_select_fusion
  1.3 0.8 copy.11
  2.1 0.1 reshape.27
  2.2 0.0 copy-start.3
  2.2 1.0 copy-done.3
  3.2 0.0 copy-start.4
  3.2 1.0 copy-done.4
  4.3 20.1 %head_in.1 = (bf16[512,1024]{1,0:T(8,128)(2,1)S(1)}, s32[16,8,128]{2,1,0:T(8,128)S(1)}) custom-call(bf16[256,1024]{1,0:T(8,128)(2,1)S(1)} %copy-done.3, bf16[256,1024]{1,0:T(8,128)(2,1)S(1)} %copy-done.4, s32[8,128]{1,0:T(8,128)S(1)} %broadcast_in_dim.16.ids), custom_call_target="tpu_custom_call" | custom-call | tf_op jit(solution)/shard_map/head_in/pallas_call | solution.py:375
  24.4 0.1 fusion.2.served
  24.5 0.6 gather_fusion.1
  25.1 0.0 copy-start.1
  25.1 0.0 copy-start.2
  25.1 2.0 %gather_fusion = bf16[16,64,1024]{2,1,0:T(8,128)(2,1)} fusion(bf16[8,64,1024]{2,1,0:T(8,128)(2,1)S(1)} %bitcast.7, s32[1024]{0:T(1024)S(1)} %pad_clamp_fusion.1), kind=kCustom, calls=%fused_computation | custom fusion | bytes 4194368 | tf_op jit(solution)/shard_map/jit(_take)/gather | solution.py:389
  27.1 0.0 copy-done.1
  27.1 0.0 copy-done.2
  27.2 60.0 %fetch.1 = (bf16[512,512]{1,0:T(8,128)(2,1)S(1)}, bf16[512,512]{1,0:T(8,128)(2,1)S(1)}, bf16[16,64,1024]{2,1,0:T(8,128)(2,1)S(1)}, bf16[2,64,1024]{2,1,0:T(8,128)(2,1)S(1)}, bf16[4,32,1024]{2,1,0:T(8,128)(2,1)S(1)}) custom-call(s32[2]{0:T(128)S(1)} %get-tuple-element.49.owners, bf16[256,1024]{1,0:T(8,128)(2,1)S(1)} %copy-done.1, ...), custom_call_target="tpu_custom_call" | custom-call | tf_op jit(solution)/shard_map/fetch/pallas_call | solution.py:403
  87.1 0.0 copy-start
  87.2 1.3 copy-done
  88.5 16.9 %attend.1 = (bf16[512,512]{1,0:T(8,128)(2,1)S(1)}, bf16[512,512]{1,0:T(8,128)(2,1)S(1)}, f32[640,1024]{1,0:T(8,128)}, bf16[2,64,1024]{2,1,0:T(8,128)(2,1)S(1)}, ...) custom-call(s32[16]{0:T(128)S(1)} %and_select_fusion.2.slots, bf16[512,512]{1,0:T(8,128)(2,1)S(1)} %get-tuple-element.28.qh, ...), custom_call_target="tpu_custom_call" | custom-call | tf_op jit(solution)/shard_map/attend/pallas_call | solution.py:413
  105.4 60.5 %give_back.1 = (bf16[256,1024]{1,0:T(8,128)(2,1)S(1)}, bf16[256,1024]{1,0:T(8,128)(2,1)S(1)}, bf16[16,64,1024]{2,1,0:T(8,128)(2,1)S(1)}, bf16[2,64,1024]{2,1,0:T(8,128)(2,1)S(1)}, bf16[4,32,1024]{2,1,0:T(8,128)(2,1)S(1)}) custom-call(bf16[512,512]{1,0:T(8,128)(2,1)S(1)} %get-tuple-element.33.att, bf16[512,512]{1,0:T(8,128)(2,1)S(1)} %get-tuple-element.34.qg, ...), custom_call_target="tpu_custom_call" | custom-call | tf_op jit(solution)/shard_map/give_back/pallas_call | solution.py:429
  165.8 2.4 %sum_owned.1 = (bf16[512,512]{1,0:T(8,128)(2,1)S(1)}, bf16[512,512]{1,0:T(8,128)(2,1)S(1)}) custom-call(s32[16]{0:T(128)S(1)} %fusion.2.served, s32[2]{0:T(128)S(1)} %get-tuple-element.49.owners, s32[2]{0:T(128)S(1)} %get-tuple-element.48.owned_at, f32[640,1024]{1,0:T(8,128)} %get-tuple-element.40.wsum, bf16[2,64,1024]{2,1,0:T(8,128)(2,1)S(1)} %get-tuple-element.41.halos, ...), custom_call_target="tpu_custom_call" | custom-call | tf_op jit(solution)/shard_map/sum_owned/pallas_call | solution.py:438
  168.3 14.5 %head_out.1 = (bf16[256,1024]{1,0:T(8,128)(2,1)S(1)}, bf16[256,1024]{1,0:T(8,128)(2,1)S(1)}) custom-call(bf16[512,512]{1,0:T(8,128)(2,1)S(1)} %get-tuple-element.44.kg, bf16[512,512]{1,0:T(8,128)(2,1)S(1)} %get-tuple-element.45.vg), custom_call_target="tpu_custom_call" | custom-call | tf_op jit(solution)/shard_map/head_out/pallas_call | solution.py:447
  182.8 0.8 copy.16
  183.6 0.8 copy.17
  184.4 0.8 copy.18
  185.1 0.8 copy.19
  (6 shorter events, 0.0 us)
Async XLA Ops:
  2.2 1.0 copy-start.3
  3.2 1.0 copy-start.4
  25.1 2.0 %copy-start.1 = (bf16[256,1024]{1,0:T(8,128)(2,1)S(1)}, bf16[256,1024]{1,0:T(8,128)(2,1)}, u32[]{:S(2)}) copy-start(bf16[256,1024]{1,0:T(8,128)(2,1)} %query.1) | copy-start | bytes 1572868
  25.1 2.0 %copy-start.2 = (bf16[256,1024]{1,0:T(8,128)(2,1)S(1)}, bf16[256,1024]{1,0:T(8,128)(2,1)}, u32[]{:S(2)}) copy-start(bf16[256,1024]{1,0:T(8,128)(2,1)} %grad.1) | copy-start | bytes 1572868
  87.1 1.3 copy-start

commit v3 on v1

v3 whole, which is shorter than its diff:
```python
from functools import partial

import jax
import jax.numpy as jnp
from jax import lax
from jax.experimental import pallas as pl
from jax.experimental.pallas import tpu as pltpu
from jax.sharding import PartitionSpec as P

HEAD_DIM = 64
BLOCK = 64
RANDOM = 2
GLOBALS = 2
PARTS = 3 + RANDOM + GLOBALS
MASKED = -1e30
MESH = pl.DeviceIdType.MESH
VMEM = pl.BlockSpec(memory_space=pltpu.VMEM)
HBM = pl.BlockSpec(memory_space=pltpu.HBM)
SMEM = pl.BlockSpec(memory_space=pltpu.SMEM)


def params(cid):
    return pltpu.CompilerParams(
        collective_id=cid, has_side_effects=True, vmem_limit_bytes=48 * 1024 * 1024
    )


def greet(n, heads):
    s, h = lax.axis_index("seq"), lax.axis_index("head")
    barrier = pltpu.get_barrier_semaphore()
    if n > 0:

        def hello(d, c):
            pl.semaphore_signal(
                barrier, inc=1, device_id={"seq": lax.rem(s + d, n)}, device_id_type=MESH
            )
            return c

        lax.fori_loop(1, n, hello, 0)
    for d in range(1, heads):
        pl.semaphore_signal(
            barrier, inc=1, device_id={"head": lax.rem(h + d, heads)}, device_id_type=MESH
        )
    pl.semaphore_wait(barrier, max(n - 1, 0) + heads - 1)


def cols(index, width, base=0):
    return pl.ds(pl.multiple_of(base + index * width, 128), width)


def rows(index, count):
    return pl.ds(pl.multiple_of(index * count, 16), count)


def each(n, f):
    def step(d, c):
        f(d)
        return c

    lax.fori_loop(1, n, step, 0)


def remote(src, dst, send, recv, **where):
    return pltpu.make_async_remote_copy(
        src_ref=src, dst_ref=dst, send_sem=send, recv_sem=recv, device_id=where,
        device_id_type=MESH,
    )


def exchange(view, heads, send, recv, local, base):
    h = lax.axis_index("head")
    copies = []
    for d in range(1, heads):
        peer = lax.rem(h + d, heads)
        source, target = view(h, peer)
        at = base * heads + d
        copies.append(remote(source, target, send.at[at], recv.at[at], head=peer))
    source, target = view(h, h)
    return copies + [pltpu.make_async_copy(source, target, local.at[base])]


def start(copies):
    for c in copies:
        c.start()


def wait(copies):
    for c in copies:
        c.wait()


def to_heads(src, dst, tokens, width):
    return lambda a, b: (src.at[:, cols(b, width)], dst.at[rows(a, tokens), :])


def piece_in(src, dst, width, offset, size):
    nt = src.shape[0]
    return lambda a, b: (
        src.at[:, :, pl.ds(pl.multiple_of(b * width + offset, 128), size)],
        dst.at[pl.ds(a * nt, nt)],
    )


def to_tokens(src, dst, tokens, width):
    return lambda a, b: (src.at[rows(b, tokens), :], dst.at[:, cols(a, width)])


def piece_out(src, dst, tokens, width, offset, size, base):
    return lambda a, b: (
        src.at[rows(b, tokens), pl.ds(base, size)],
        dst.at[:, pl.ds(pl.multiple_of(a * width + offset, 128), size)],
    )


def kernel_in(n, heads, size, key, ids, pair, ids_all, send, recv, local, isend, irecv):
    s = lax.axis_index("seq")
    greet(n, heads)
    copies = exchange(
        piece_in(key, pair, key.shape[2] // heads, 0, size), heads, send, recv, local, 0
    )

    def idc(d):
        return remote(ids, ids_all.at[s], isend.at[d], irecv.at[d], seq=lax.rem(s + d, n))

    mine = pltpu.make_async_copy(ids, ids_all.at[s], local.at[1])
    start(copies)
    each(n, lambda d: idc(d).start())
    mine.start()
    each(n, lambda d: idc(d).wait())
    mine.wait()
    wait(copies)


def halo(n, low, high, got, send, recv, at=0):
    s = lax.axis_index("seq")
    up, down = 2 * at, 2 * at + 1
    here = pl.ds(at * low.shape[1], low.shape[1])
    return [
        remote(high, got.at[0, :, here], send.at[up], recv.at[up], seq=lax.rem(s + 1, n)),
        remote(low, got.at[1, :, here], send.at[down], recv.at[down], seq=lax.rem(s + n - 1, n)),
    ]


def far_first(n, make):
    def go(i, c):
        make(n // 2 + ((i + 1) // 2) * (2 * lax.rem(i, 2) - 1)).start()
        return c

    lax.fori_loop(0, n - 1, go, 0)


def random_piece(n, c, src_of, dst, size, send, recv):
    s = lax.axis_index("seq")

    def make(d):
        peer = lax.rem(s + d, n)
        return remote(
            src_of(peer), dst.at[s, :, pl.ds(c * size, size)], send.at[c * n + d],
            recv.at[c * n + d], seq=peer,
        )

    return make


class Shared:
    def __init__(self, n, src, here, mine, layer, done, every, sems):
        s = lax.axis_index("seq")
        gs, gr, ls, lr, fs, fr, loc = sems
        self.group = group = src.shape[0]
        self.layers = n // group
        self.me, self.level = lax.rem(s, group), s // group
        self.mine, self.layer, self.done, self.every, self.here = mine, layer, done, every, here
        self.step1 = [pltpu.make_async_copy(src.at[self.me], here.at[self.me], loc.at[0])]
        self.step3 = []
        for j in range(1, group):
            to = lax.rem(self.me + j, group)
            peer = self.level * group + to
            self.step1.append(remote(src.at[to], here.at[self.me], gs.at[j], gr.at[j], seq=peer))
            self.step3.append(remote(done, every.at[self.me], fs.at[j], fr.at[j], seq=peer))
        self.across = lambda j: remote(
            mine, layer.at[self.level], ls.at[j], lr.at[j],
            seq=lax.rem(self.level + j, self.layers) * group + self.me,
        )

    def middle(self, combine):
        wait(self.step1)
        part = combine(self.here)
        self.mine[...] = part
        self.layer[self.level] = part
        each(self.layers, lambda j: self.across(j).start())

    def finish(self, combine):
        each(self.layers, lambda j: self.across(j).wait())
        total = combine(self.layer)
        self.done[...] = total
        self.every[self.me] = total
        start(self.step3)


def kernel_fetch(n, heads, pieces, served, owners, owned_at, query, grad, key, value, first, ready,
                 qh, gh, incoming, halos, gall, *rest):
    landed, rest = (first,) + rest[: pieces - 1], rest[pieces - 1 :]
    outgoing, gsrc, ghere, gmine, glayer, gdone = rest[:6]
    send, recv, local, bs, br, hs, hr, *gsems = rest[6:]
    s = lax.axis_index("seq")
    tokens, width = query.shape[0], query.shape[1] // heads
    size = 2 * width // pieces
    nb = first.shape[0]
    half = pieces // 2
    greet(n, heads)
    moves = [[]]
    for c in range(1, pieces):
        src = key if c < half else value
        moves.append(exchange(
            piece_in(src, landed[c], width, (c % half) * size, size),
            heads, send, recv, local, c,
        ))
    blocks = [
        random_piece(n, c, (lambda p, c=c: (ready.at[p] if c == 0 else outgoing.at[c - 1, p])),
                     incoming, size, bs, br)
        for c in range(pieces)
    ]
    qmove = exchange(to_heads(query, qh, tokens, width), heads, send, recv, local, pieces)
    qmove += exchange(to_heads(grad, gh, tokens, width), heads, send, recv, local, pieces + 1)
    edges = []
    for c in range(pieces):
        edges += halo(n, landed[c].at[0], landed[c].at[nb - 1], halos, hs, hr, c)
    shared = Shared(n, gsrc, ghere, gmine, glayer, gdone, gall, gsems)
    for m in moves:
        start(m)
    far_first(n, blocks[0])
    start(qmove)
    keep = pltpu.make_async_copy(ready.at[s], incoming.at[s, :, pl.ds(0, size)],
                                 local.at[pieces + 2])
    keep.start()
    for c in range(1, pieces):
        wait(moves[c])
        at = pl.ds(c * size, size)

        def gather(i, carry):
            outgoing[c - 1, i] = landed[c][served[i]]
            return carry

        lax.fori_loop(0, n, gather, 0)
        incoming[s, :, at] = landed[c][served[s]]
        if c == pieces - 1:
            group = gsrc.shape[0]
            per = group // GLOBALS
            count = BLOCK // per
            for m in range(group):
                low = (m % per) * count
                for k in range(pieces):
                    gsrc[m, :, pl.ds(k * size, size)] = landed[k][
                        owned_at[m // per], pl.ds(low, count), :
                    ]
            start(shared.step1 + edges)
            mine = owners[shared.me * GLOBALS // group]
            shared.middle(lambda ref: ref[lax.rem(mine, group)])
        far_first(n, blocks[c])
    shared.finish(lambda ref: ref[mine // group])
    keep.wait()
    wait(edges + qmove + shared.step3)
    for c in range(pieces):
        each(n, lambda d: blocks[c](d).wait())


def kernel_return(n, heads, pieces, served, owners, owned_at, att, qg, sending, edge, gsend, wsum,
                  out, qout, kout, vout, returned, halos, gall, summed, ghere, gmine, glayer,
                  gdone, send, recv, local, bs, br, hs, hr, *gsems):
    s = lax.axis_index("seq")
    width = att.shape[1]
    tokens = att.shape[0] // heads
    nb = att.shape[0] // BLOCK
    size = 2 * width // pieces
    half = pieces // 2
    greet(n, heads)
    moves = [
        exchange(
            piece_out(summed, kout if c < half else vout, tokens, width, (c % half) * size, size,
                      c * size),
            heads, send, recv, local, c,
        )
        for c in range(pieces)
    ]
    blocks = [
        random_piece(n, c, lambda p, c=c: sending.at[p, :, pl.ds(c * size, size)], returned, size,
                     bs, br)
        for c in range(pieces)
    ]
    qmove = exchange(to_tokens(att, out, tokens, width), heads, send, recv, local, pieces)
    qmove += exchange(to_tokens(qg, qout, tokens, width), heads, send, recv, local, pieces + 1)
    edges = halo(n, edge.at[0], edge.at[1], halos, hs, hr)
    shared = Shared(n, gsend, ghere, gmine, glayer, gdone, gall, gsems)
    keep = pltpu.make_async_copy(sending.at[s], returned.at[s], local.at[pieces + 2])

    def combine(ref):
        def add(i, acc):
            return acc + ref[i].astype(jnp.float32)

        zero = jnp.zeros(ref.shape[1:], jnp.float32)
        return lax.fori_loop(0, ref.shape[0], add, zero).astype(jnp.bfloat16)

    start(shared.step1 + edges)
    far_first(n, blocks[0])
    start(qmove + [keep])
    shared.middle(combine)
    for c in range(1, pieces):
        far_first(n, blocks[c])
    shared.finish(combine)
    keep.wait()
    wait(edges + shared.step3)
    strip = 16
    per = shared.group // GLOBALS
    count = BLOCK // per

    def weight(cond):
        return jnp.where(cond, 1.0, 0.0).astype(jnp.float32)

    for c in range(pieces):
        each(n, lambda d: blocks[c](d).wait())
        at = pl.ds(c * size, size)

        def one_strip(t, carry):
            low = pl.multiple_of(t * strip, strip)
            here = pl.ds(low, strip)
            acc = [wsum[pl.ds(pl.multiple_of((j + 1) * BLOCK + low, strip), strip), at]
                   for j in range(nb)]
            acc[0] = acc[0] + halos[0, here, at].astype(jnp.float32)
            acc[-1] = acc[-1] + halos[1, here, at].astype(jnp.float32)
            for g in range(GLOBALS):
                inside = pl.ds(pl.multiple_of(lax.rem(low, count), strip), strip)
                extra = gall[g * per + low // count, inside, at].astype(jnp.float32)
                for j in range(nb):
                    hit = (owners[g] == s) & (owned_at[g] == j)
                    acc[j] = acc[j] + weight(hit) * extra

            def add(i, accs):
                x = returned[i, here, at].astype(jnp.float32)
                which = served[i]
                return tuple(accs[j] + weight(which == j) * x for j in range(nb))

            acc = lax.fori_loop(0, n, add, tuple(acc))
            for j in range(nb):
                summed[pl.ds(pl.multiple_of(j * BLOCK + low, strip), strip), at] = acc[j].astype(
                    jnp.bfloat16
                )
            return carry

        lax.fori_loop(0, BLOCK // strip, one_strip, 0)
        start(moves[c])
    wait(qmove)
    for m in moves:
        wait(m)


def dot(a, b, ca, cb):
    return lax.dot_general(a, b, (((ca,), (cb,)), ((), ())), preferred_element_type=jnp.float32)


def kernel_attend(n, lanes, pieces, slots, qh, gh, halos, incoming, gall, *rest):
    landed, rest = rest[:pieces], rest[pieces:]
    att, qg, wsum, edge, sending, gsum, pairs, keys, gacc = rest
    nb = qh.shape[0] // BLOCK
    width = qh.shape[1]
    s = lax.axis_index("seq")
    per = lanes // HEAD_DIM
    scale = jnp.asarray(HEAD_DIM ** (-0.5), jnp.bfloat16)
    pairs[pl.ds(0, BLOCK)] = halos[0]
    size = landed[0].shape[1]
    for c in range(pieces):
        pairs[pl.ds(BLOCK, nb * BLOCK), pl.ds(c * size, size)] = landed[c][...]
    pairs[pl.ds((nb + 1) * BLOCK, BLOCK)] = halos[1]
    keys[pl.ds((3 + RANDOM) * BLOCK, GLOBALS * BLOCK)] = gall[...]
    gacc[...] = jnp.zeros_like(gacc)
    wsum[...] = jnp.zeros_like(wsum)
    if n > RANDOM * nb:
        sending[...] = jnp.zeros_like(sending)
    lane_head = lax.broadcasted_iota(jnp.int32, (BLOCK, lanes), 1) // HEAD_DIM
    part = lax.broadcasted_iota(jnp.int32, (PARTS * BLOCK, 1), 0) // BLOCK

    def stack(x):
        zero = jnp.zeros_like(x)
        return jnp.concatenate([jnp.where(lane_head == j, x, zero) for j in range(per)], axis=0)

    def unstack(x):
        got = x[0:BLOCK]
        for j in range(1, per):
            got = jnp.where(lane_head == j, x[j * BLOCK : (j + 1) * BLOCK], got)
        return got

    def block(b, carry):
        here = pl.ds(pl.multiple_of(b * BLOCK, BLOCK), BLOCK)
        window = pl.ds(pl.multiple_of(b * BLOCK, BLOCK), 3 * BLOCK)
        keys[pl.ds(0, 3 * BLOCK)] = pairs[window]
        for r in range(RANDOM):
            keys[pl.ds((3 + r) * BLOCK, BLOCK)] = incoming[slots[b * RANDOM + r]]
        number = s * nb + b
        bad = ((part == 0) & (number == 0)) | ((part == 2) & (number == n * nb - 1))
        for g in range(width // lanes):
            at = pl.ds(g * lanes, lanes)
            vat = pl.ds(width + g * lanes, lanes)
            q = stack(qh[here, at]) * scale
            do = stack(gh[here, at])
            k = keys[:, at]
            v = keys[:, vat]
            scores = jnp.where(bad, MASKED, dot(k, q, 1, 1))
            raw = jnp.exp(scores - jnp.max(scores, axis=0, keepdims=True))
            probs = raw * (1.0 / jnp.sum(raw, axis=0, keepdims=True))
            half = probs.astype(jnp.bfloat16)
            pgrad = dot(v, do, 1, 1)
            delta = jnp.sum(half.astype(jnp.float32) * pgrad, axis=0, keepdims=True)
            ds = (probs * (pgrad - delta)).astype(jnp.bfloat16)
            att[here, at] = unstack(dot(half, v, 0, 0)).astype(jnp.bfloat16)
            qg[here, at] = (unstack(dot(ds, k, 0, 0)) * HEAD_DIM ** (-0.5)).astype(jnp.bfloat16)
            for x, y, to in ((ds, q, at), (half, do, vat)):
                grad = dot(x, y, 1, 0)
                wsum[window, to] += grad[: 3 * BLOCK]
                for r in range(RANDOM):
                    low = (3 + r) * BLOCK
                    sending[slots[b * RANDOM + r], :, to] = grad[low : low + BLOCK].astype(
                        jnp.bfloat16
                    )
                gacc[:, to] += grad[(3 + RANDOM) * BLOCK :]
        return carry

    lax.fori_loop(0, nb, block, 0)
    edge[0] = wsum[pl.ds(0, BLOCK)].astype(jnp.bfloat16)
    edge[1] = wsum[pl.ds((nb + 1) * BLOCK, BLOCK)].astype(jnp.bfloat16)
    gsum[...] = gacc[...].astype(jnp.bfloat16)


def body(n, heads, query_rows, key_rows, value_rows, out_grad, random_blocks, global_blocks):
    bf = jnp.bfloat16
    tokens, full = query_rows.shape
    width = full // heads
    total = tokens * heads
    nb = total // BLOCK
    me = lax.axis_index("seq")
    dma = pltpu.SemaphoreType.DMA
    sds = jax.ShapeDtypeStruct
    requests = RANDOM * nb
    flat = random_blocks.reshape(requests)
    ids = jnp.broadcast_to(jnp.pad(flat, (0, 128 - requests))[None], (8, 128))
    pieces = min(4, 2 * width // 128)
    size = 2 * width // pieces
    blocked = (tokens // BLOCK, BLOCK, full)
    key_blocks, value_blocks = key_rows.reshape(blocked), value_rows.reshape(blocked)
    first, ids_all = pl.pallas_call(
        partial(kernel_in, n, heads, size),
        out_shape=(sds((nb, BLOCK, size), bf), sds((n, 8, 128), jnp.int32)),
        in_specs=[HBM, VMEM],
        out_specs=(VMEM,) * 2,
        scratch_shapes=[dma((heads,)), dma((heads,)), dma((2,)), dma((n,)), dma((n,))],
        compiler_params=params(0),
        name="head_in",
    )(key_blocks, ids)
    asked = ids_all[:, 0, :requests]
    served = jnp.sum(jnp.where(asked // nb == me, asked % nb, 0), axis=1).astype(jnp.int32)
    owners = global_blocks // nb
    owned_at = global_blocks % nb
    ready = jnp.take(first, served, axis=0, mode="clip")
    group = 4
    layers = n // group
    chunk = GLOBALS * BLOCK // group
    slab = sds((n, BLOCK, 2 * width), bf)
    small = sds((group, chunk, 2 * width), bf)
    wide = (chunk, 2 * width)
    scratch = [
        pltpu.VMEM(small.shape, bf), pltpu.VMEM(wide, bf), pltpu.VMEM((layers,) + wide, bf),
        pltpu.VMEM(wide, bf),
        dma(((pieces + 2) * heads,)), dma(((pieces + 2) * heads,)), dma((pieces + 3,)),
        dma((pieces * n,)), dma((pieces * n,)), dma((2 * pieces,)), dma((2 * pieces,)),
        dma((group,)), dma((group,)), dma((layers,)), dma((layers,)), dma((group,)),
        dma((group,)), dma((1,)),
    ]
    edges = sds((2, BLOCK, 2 * width), bf)
    qh, gh, incoming, halos, gall, *landed = pl.pallas_call(
        partial(kernel_fetch, n, heads, pieces),
        out_shape=(sds((total, width), bf), sds((total, width), bf), slab, edges, small)
        + (sds((nb, BLOCK, size), bf),) * (pieces - 1),
        in_specs=[SMEM] * 3 + [HBM] * 4 + [VMEM] * 2,
        out_specs=(VMEM,) * (4 + pieces),
        scratch_shapes=[pltpu.VMEM((pieces - 1, n, BLOCK, size), bf), pltpu.VMEM(small.shape, bf)]
        + scratch,
        compiler_params=params(1),
        name="fetch",
    )(served, owners, owned_at, query_rows, out_grad, key_blocks, value_blocks, first, ready)
    gwide = (GLOBALS * BLOCK, 2 * width)
    att, qg, wsum, edge, sending, gsum = pl.pallas_call(
        partial(kernel_attend, n, min(256, width), pieces),
        out_shape=(
            sds((total, width), bf), sds((total, width), bf),
            sds(((nb + 2) * BLOCK, 2 * width), jnp.float32), edges, slab, sds(gwide, bf),
        ),
        in_specs=[SMEM] + [VMEM] * (5 + pieces),
        out_specs=(VMEM,) * 6,
        scratch_shapes=[
            pltpu.VMEM(((nb + 2) * BLOCK, 2 * width), bf),
            pltpu.VMEM((PARTS * BLOCK, 2 * width), bf),
            pltpu.VMEM(gwide, jnp.float32),
        ],
        compiler_params=pltpu.CompilerParams(vmem_limit_bytes=48 * 1024 * 1024),
        name="attend",
    )(flat // nb, qh, gh, halos, incoming, gall.reshape(gwide),
      *[x.reshape(total, size) for x in (first, *landed)])
    return pl.pallas_call(
        partial(kernel_return, n, heads, pieces),
        out_shape=(sds((tokens, full), bf),) * 4,
        in_specs=[SMEM] * 3 + [VMEM] * 6,
        out_specs=(VMEM,) * 4,
        scratch_shapes=[
            pltpu.VMEM(slab.shape, bf), pltpu.VMEM(edges.shape, bf), pltpu.VMEM(small.shape, bf),
            pltpu.VMEM((total, 2 * width), bf),
        ] + scratch,
        compiler_params=params(2),
        name="give_back",
    )(served, owners, owned_at, att, qg, sending, edge, gsum.reshape(group, chunk, 2 * width),
      wsum)


def solution(mesh):
    rows_spec = P(("seq", "head"), None)
    return jax.shard_map(
        partial(body, mesh.shape["seq"], mesh.shape["head"]),
        mesh=mesh,
        in_specs=(rows_spec,) * 4 + (P("seq", None), P()),
        out_specs=(rows_spec,) * 4,
        check_vma=False,
    )
```

time: 195 us -> 166 us (0.85)
  Pallas kernels: 183 us -> 153 us
    pallas_call x6 -> x4, Pallas kernels: 183 us -> 153 us  [the longest x1 64.6 us: body(): pl.pallas_call(partial(kernel_return, n, heads, pieces), out_shape=(sds((...]
    unnamed x15 -> x17, local copies, waits for them, and re-layouts: 7.35 us -> 10.7 us
    gather x2 -> x1, local copies, waits for them, and re-layouts: 2.59 us -> 0.58 us  [body(): ready = jnp.take(first, served, axis=0, mode='clip')]
where the time goes in v3:
time: 166 us
  Pallas kernels  153 us (92%)
  local copies, waits for them, and re-layouts  11.4 us (7%)
    pallas_call x1, Pallas kernels, body(): pl.pallas_call(partial(kernel_return, n, heads, pieces), out_shape=(sds((...  64.6 us
    pallas_call x1, Pallas kernels, body(): pl.pallas_call(partial(kernel_fetch, n, heads, pieces), out_shape=(sds((t...  59.5 us
    pallas_call x1, Pallas kernels, body(): pl.pallas_call(partial(kernel_attend, n, min(256, width), pieces), out_sh...  17 us
    pallas_call x1, Pallas kernels, body(): pl.pallas_call(partial(kernel_in, n, heads, size), out_shape=(sds((nb, BL...  11.6 us
    unnamed x17, local copies, waits for them, and re-layouts  10.7 us

profile of v3, /device:TPU:0, one launch (start us, length us, event | category | flops | bytes accessed | tf_op | source)
XLA Modules:
  0.0 165.6 jit_solution(3110720556785795945)
XLA Ops:
  0.6 0.7 and_select_fusion.1
  1.3 0.8 copy.11
  2.1 0.1 reshape.37
  2.2 0.0 copy-start.1
  2.2 1.0 copy-done.1
  3.2 11.6 %head_in.1 = (bf16[8,64,256]{2,1,0:T(8,128)(2,1)S(1)}, s32[16,8,128]{2,1,0:T(8,128)S(1)}) custom-call(bf16[4,64,1024]{2,1,0:T(8,128)(2,1)S(1)} %bitcast.10, s32[8,128]{1,0:T(8,128)S(1)} %broadcast_in_dim.12.ids), custom_call_target="tpu_custom_call" | custom-call | tf_op jit(solution)/shard_map/head_in/pallas_call | solution.py:448
  14.9 0.1 fusion.2.served
  15.0 0.6 gather_fusion
  15.6 0.0 copy-start.2
  15.6 1.0 copy-done.2
  16.6 0.0 copy-start.3
  16.6 1.0 copy-done.3
  17.7 0.0 copy-start.4
  17.7 1.0 copy-done.4
  18.7 0.0 copy-start.5
  18.7 1.0 copy-done.5
  19.8 59.5 %fetch.1 = (bf16[512,512]{1,0:T(8,128)(2,1)S(1)}, bf16[512,512]{1,0:T(8,128)(2,1)S(1)}, bf16[16,64,1024]{2,1,0:T(8,128)(2,1)}, bf16[2,64,1024]{2,1,0:T(8,128)(2,...) custom-call(s32[16]{0:T(128)S(1)} %fusion.2.served, ...), custom_call_target="tpu_custom_call" | custom-call | tf_op jit(solution)/shard_map/fetch/pallas_call | solution.py:477
  79.3 17.0 %attend.1 = (bf16[512,512]{1,0:T(8,128)(2,1)S(1)}, bf16[512,512]{1,0:T(8,128)(2,1)S(1)}, f32[640,1024]{1,0:T(8,128)}, bf16[2,64,1024]{2,1,0:T(8,128)(2,1)S(1)}, ...) custom-call(s32[16]{0:T(128)S(1)} %and_select_fusion.slots, bf16[512,512]{1,0:T(8,128)(2,1)S(1)} %get-tuple-element.22.qh, ...), custom_call_target="tpu_custom_call" | custom-call | tf_op jit(solution)/shard_map/attend/pallas_call | solution.py:489
  96.2 0.0 copy-start
  96.2 1.6 copy-done
  97.8 64.6 %give_back.1 = (bf16[256,1024]{1,0:T(8,128)(2,1)S(1)}, bf16[256,1024]{1,0:T(8,128)(2,1)S(1)}, bf16[256,1024]{1,0:T(8,128)(2,1)S(1)}, bf16[256,1024]{1,0:T(8,128)(2,1)S(1)}) custom-call(s32[16]{0:T(128)S(1)} %fusion.2.served, s32[2]{0:T(128)S(1)} %get-tuple-element.37.owners, s32[2]{0:T(128)S(1)} %get-tuple-element.36.owned_at, ...), custom_call_target="tpu_custom_call" | custom-call | tf_op jit(solution)/shard_map/give_back/pallas_call | solution.py:506
  162.4 0.8 copy.16
  163.2 0.8 copy.17
  164.0 0.8 copy.18
  164.8 0.8 copy.19
  (5 shorter events, 0.0 us)
Async XLA Ops:
  2.2 1.0 copy-start.1
  15.6 1.0 copy-start.2
  16.6 1.0 copy-start.3
  17.7 1.0 copy-start.4
  18.7 1.0 copy-start.5
  96.2 1.6 copy-start

commit v4 on v3

--- a/solution.py
+++ b/solution.py
@@ -21,7 +21,7 @@
 
 def params(cid):
     return pltpu.CompilerParams(
-        collective_id=cid, has_side_effects=True, vmem_limit_bytes=48 * 1024 * 1024
+        collective_id=cid, has_side_effects=True, vmem_limit_bytes=24 * 1024 * 1024
     )
 
 
@@ -423,10 +423,19 @@
                 gacc[:, to] += grad[(3 + RANDOM) * BLOCK :]
         return carry
 
-    lax.fori_loop(0, nb, block, 0)
+    lax.fori_loop(0, nb, block, 0, unroll=2)
     edge[0] = wsum[pl.ds(0, BLOCK)].astype(jnp.bfloat16)
     edge[1] = wsum[pl.ds((nb + 1) * BLOCK, BLOCK)].astype(jnp.bfloat16)
     gsum[...] = gacc[...].astype(jnp.bfloat16)
+
+
+def kernel_store(a, b, c, d, wa, wb, wc, wd, sem):
+    copies = [
+        pltpu.make_async_copy(x, y, sem.at[i])
+        for i, (x, y) in enumerate(((a, wa), (b, wb), (c, wc), (d, wd)))
+    ]
+    start(copies)
+    wait(copies)
 
 
 def body(n, heads, query_rows, key_rows, value_rows, out_grad, random_blocks, global_blocks):
@@ -445,6 +454,10 @@
     size = 2 * width // pieces
     blocked = (tokens // BLOCK, BLOCK, full)
     key_blocks, value_blocks = key_rows.reshape(blocked), value_rows.reshape(blocked)
+    query_rows, key_blocks, value_blocks, out_grad = (
+        pltpu.with_memory_space_constraint(x, pltpu.HBM)
+        for x in (query_rows, key_blocks, value_blocks, out_grad)
+    )
     first, ids_all = pl.pallas_call(
         partial(kernel_in, n, heads, size),
         out_shape=(sds((nb, BLOCK, size), bf), sds((n, 8, 128), jnp.int32)),
@@ -499,11 +512,11 @@
             pltpu.VMEM((PARTS * BLOCK, 2 * width), bf),
             pltpu.VMEM(gwide, jnp.float32),
         ],
-        compiler_params=pltpu.CompilerParams(vmem_limit_bytes=48 * 1024 * 1024),
+        compiler_params=pltpu.CompilerParams(vmem_limit_bytes=24 * 1024 * 1024),
         name="attend",
     )(flat // nb, qh, gh, halos, incoming, gall.reshape(gwide),
       *[x.reshape(total, size) for x in (first, *landed)])
-    return pl.pallas_call(
+    results = pl.pallas_call(
         partial(kernel_return, n, heads, pieces),
         out_shape=(sds((tokens, full), bf),) * 4,
         in_specs=[SMEM] * 3 + [VMEM] * 6,
@@ -516,6 +529,15 @@
         name="give_back",
     )(served, owners, owned_at, att, qg, sending, edge, gsum.reshape(group, chunk, 2 * width),
       wsum)
+    return pl.pallas_call(
+        kernel_store,
+        out_shape=(sds((tokens, full), bf),) * 4,
+        in_specs=[VMEM] * 4,
+        out_specs=(HBM,) * 4,
+        scratch_shapes=[dma((4,))],
+        compiler_params=pltpu.CompilerParams(vmem_limit_bytes=16 * 1024 * 1024),
+        name="store",
+    )(*results)
 
 
 def solution(mesh):

time: 166 us -> 151 us (0.910)
  local copies, waits for them, and re-layouts: 11.4 us -> 1.43 us
  Pallas kernels: 153 us -> 148 us
    unnamed x17 -> x1, local copies, waits for them, and re-layouts: 10.7 us -> 0.75 us
    pallas_call x1, Pallas kernels: 17 us -> 13 us  [body(): pl.pallas_call(partial(kernel_attend, n, min(256, width), pieces), out_sh...]
where the time goes in v4:
time: 151 us
  Pallas kernels  148 us (98%)
    pallas_call x1, Pallas kernels, body(): pl.pallas_call(partial(kernel_return, n, heads, pieces), out_shape=(sds((...  63.4 us
    pallas_call x1, Pallas kernels, body(): pl.pallas_call(partial(kernel_fetch, n, heads, pieces), out_shape=(sds((t...  58.1 us
    pallas_call x1, Pallas kernels, body(): pl.pallas_call(partial(kernel_attend, n, min(256, width), pieces), out_sh...  13 us
    pallas_call x1, Pallas kernels, body(): pl.pallas_call(partial(kernel_in, n, heads, size), out_shape=(sds((nb, BL...  11.9 us

profile of v4, /device:TPU:0, one launch (start us, length us, event | category | flops | bytes accessed | tf_op | source)
XLA Modules:
  0.0 150.7 jit_solution(7294747845570402407)
XLA Ops:
  0.6 0.7 and_select_fusion.1
  1.3 0.8 copy.11
  2.1 0.1 reshape.37
  2.2 11.9 %head_in.1 = (bf16[8,64,256]{2,1,0:T(8,128)(2,1)S(1)}, s32[16,8,128]{2,1,0:T(8,128)S(1)}) custom-call(bf16[4,64,1024]{2,1,0:T(8,128)(2,1)} %bitcast.15, s32[8,128]{1,0:T(8,128)S(1)} %broadcast_in_dim.12.ids), custom_call_target="tpu_custom_call" | custom-call | tf_op jit(solution)/shard_map/head_in/pallas_call | solution.py:461
  14.1 0.1 fusion.2.served
  14.2 0.6 gather_fusion
  14.8 58.1 %fetch.1 = (bf16[512,512]{1,0:T(8,128)(2,1)S(1)}, bf16[512,512]{1,0:T(8,128)(2,1)S(1)}, bf16[16,64,1024]{2,1,0:T(8,128)(2,1)S(1)}, bf16[2,64,1024]{2,1,0:T(8,128...) custom-call(s32[16]{0:T(128)S(1)} %fusion.2.served, ...), custom_call_target="tpu_custom_call" | custom-call | tf_op jit(solution)/shard_map/fetch/pallas_call | solution.py:490
  72.9 13.0 %attend.1 = (bf16[512,512]{1,0:T(8,128)(2,1)S(1)}, bf16[512,512]{1,0:T(8,128)(2,1)S(1)}, f32[640,1024]{1,0:T(8,128)S(1)}, bf16[2,64,1024]{2,1,0:T(8,128)(2,1)S(1...) custom-call(s32[16]{0:T(128)S(1)} %and_select_fusion.slots, ...), custom_call_target="tpu_custom_call" | custom-call | tf_op jit(solution)/shard_map/attend/pallas_call | solution.py:502
  85.9 63.4 %give_back.1 = (bf16[256,1024]{1,0:T(8,128)(2,1)S(1)}, bf16[256,1024]{1,0:T(8,128)(2,1)S(1)}, bf16[256,1024]{1,0:T(8,128)(2,1)S(1)}, bf16[256,1024]{1,0:T(8,128)(2,1)S(1)}) custom-call(s32[16]{0:T(128)S(1)} %fusion.2.served, s32[2]{0:T(128)S(1)} %get-tuple-element.45.owners, s32[2]{0:T(128)S(1)} %get-tuple-element.44.owned_at, ...), custom_call_target="tpu_custom_call" | custom-call | tf_op jit(solution)/shard_map/give_back/pallas_call | solution.py:519
  149.3 1.3 store.1
  (5 shorter events, 0.0 us)
